TPU v7x, 32 devices: a whole 2x2x4 slice. The times are simulated.
32 devices in a mesh: grp: 2 (over x), gz: 8 (over z, y), col: 2 (over core).
Axes of the slice: x: 2, y: 2, z: 4, core: 2. Of those that a mesh axis runs over, the one named last changes fastest.
Arguments:
- noisy_image: float32 [4, 1024, 768], P('grp', 'gz', 'col'), parts along dimension 0, may hold values from -6 to 6
- fresh_noise: float32 [4, 1024, 768], P('grp', 'gz', 'col'), parts along dimension 0, may hold values from -6 to 6
- coil_maps: float32 [8, 4, 1024, 768], P('col', 'grp', 'gz'), parts along dimension 1, may hold values from -1.5 to 1.5
- measured: float32 [4, 768, 8, 1024], P('grp', 'gz', 'col'), parts along dimension 0, may hold values from -2.4 to 2.4
- sampled: int32 [768, 2048], P('gz', 'grp'), parts along dimension 1, may hold values 0 or 1
- first_kernel: bfloat16 [9, 64, 2], replicated, may hold values from -1.5 to 1.5
- inner_kernels: bfloat16 [1, 9, 64, 64], replicated, may hold values from -0.25 to 0.25
- last_kernel: bfloat16 [9, 2, 64], replicated, may hold values from -0.25 to 0.25
Outputs:
- next_image: float32 [4, 1024, 768], P('grp', 'gz', 'col'), parts along dimension 0
There are 2 independent parts, one for each index of `grp`. A program takes and returns all parts, laid end to end along the dimension named above; an argument that names none is the same for every part. Nothing has to cross between parts.
All inputs are finite; a program needn't handle non-finite values. No bound on the sum of `sampled` on one device may be relied on, other than what follows from the above.
Results may differ from a plain program's by a relative error of at most 0.00044.
Values may be sent and summed in bfloat16 or wider, within the bound.
No kernel may reach another device: no remote copies, remote signals or barrier semaphores. Data moves between devices by JAX's collectives and lax.ppermute only.
A program may use at most 128 MiB of HBM per device.

v0:
```python
from functools import partial
import math

import jax
import jax.numpy as jnp
from jax import lax
from jax.sharding import PartitionSpec as P

H_FAC = 8
W_FAC = 6


SCALE_NOW = 0.8
SIGMA_NOW = 0.6
STEP_GAIN = 1.0
SCALE_NEXT = 0.9
DIRECT_GAIN = 0.31622776601683794
NOISE_GAIN = 0.3


def with_halo(block, sides, width):
    for axis, dim in sides:
        count = lax.axis_size(axis)
        forward = [(i, i + 1) for i in range(count - 1)]
        backward = [(target, source) for source, target in forward]
        low = lax.ppermute(
            lax.slice_in_dim(block, block.shape[dim] - width, None, axis=dim), axis, forward
        )
        high = lax.ppermute(lax.slice_in_dim(block, 0, width, axis=dim), axis, backward)
        block = jnp.concatenate([low, block, high], axis=dim)
    return block


def convolve_padded(padded, kernel):
    kernel_out = kernel.shape[1]
    kernel_in = kernel.shape[2]
    filters = jnp.transpose(kernel.reshape(3, 3, kernel_out, kernel_in), (2, 3, 0, 1))
    result = lax.conv_general_dilated(
        padded[None],
        filters,
        (1, 1),
        "VALID",
        dimension_numbers=("NCHW", "OIHW", "NCHW"),
        preferred_element_type=jnp.float32,
    )
    return result[0]


def tile_layer(features, kernel):
    padded = with_halo(features, (("gz", 1), ("col", 2)), 1)
    return convolve_padded(padded, kernel)


def network(features, first_kernel, inner_kernels, last_kernel, layer_fn):
    hidden = jax.nn.silu(layer_fn(features.astype(jnp.bfloat16), first_kernel)).astype(jnp.bfloat16)
    hidden = jax.nn.silu(layer_fn(hidden, inner_kernels[0])).astype(jnp.bfloat16)
    return layer_fn(hidden, last_kernel)


def rotation(rows_len, cols_len, modulus, direction):
    first_index = jnp.arange(rows_len, dtype=jnp.int32)
    second_index = jnp.arange(cols_len, dtype=jnp.int32)
    phase_index = first_index[:, None] * second_index[None, :] % modulus
    angles = phase_index.astype(jnp.float32) * (direction * 2.0 * math.pi / modulus)
    return (jnp.cos(angles), jnp.sin(angles))


def complex_dot(matrix_pair, data_pair, contracting):
    product = partial(
        lax.dot_general,
        dimension_numbers=(contracting, ((), ())),
        precision=lax.Precision.HIGHEST,
        preferred_element_type=jnp.float32,
    )
    return (
        product(matrix_pair[0], data_pair[0]) - product(matrix_pair[1], data_pair[1]),
        product(matrix_pair[0], data_pair[1]) + product(matrix_pair[1], data_pair[0]),
    )


def complex_mul(first_pair, second_pair):
    return (
        first_pair[0] * second_pair[0] - first_pair[1] * second_pair[1],
        first_pair[0] * second_pair[1] + first_pair[1] * second_pair[0],
    )


def transform_last(data_pair, outer_len, direction):
    vectors, length = data_pair[0].shape
    inner_len = length // outer_len
    shaped = (
        data_pair[0].reshape(vectors, outer_len, inner_len),
        data_pair[1].reshape(vectors, outer_len, inner_len),
    )
    sectioned = complex_dot(
        rotation(outer_len, outer_len, outer_len, direction), shaped, ((1,), (1,))
    )
    twiddles = rotation(outer_len, inner_len, length, direction)
    twisted = complex_mul(sectioned, (twiddles[0][:, None, :], twiddles[1][:, None, :]))
    finished = complex_dot(
        rotation(inner_len, inner_len, inner_len, direction), twisted, ((1,), (2,))
    )
    factor = 1.0 / math.sqrt(length)
    return (
        finished[0].reshape(length, vectors) * factor,
        finished[1].reshape(length, vectors) * factor,
    )


def transform_first(data_pair, outer_len, direction):
    length, vectors = data_pair[0].shape
    inner_len = length // outer_len
    shaped = (
        data_pair[0].reshape(outer_len, inner_len, vectors),
        data_pair[1].reshape(outer_len, inner_len, vectors),
    )
    sectioned = complex_dot(
        rotation(outer_len, outer_len, outer_len, direction), shaped, ((1,), (0,))
    )
    twiddles = rotation(outer_len, inner_len, length, direction)
    twisted = complex_mul(sectioned, (twiddles[0][:, :, None], twiddles[1][:, :, None]))
    finished = complex_dot(
        rotation(inner_len, inner_len, inner_len, direction), twisted, ((1,), (1,))
    )
    factor = 1.0 / math.sqrt(length)
    return (
        finished[0].reshape(length, vectors) * factor,
        finished[1].reshape(length, vectors) * factor,
    )


def local(
    noisy_image, fresh_noise, coil_maps, measured, sampled, first_kernel, inner_kernels, last_kernel
):
    predicted = network(noisy_image, first_kernel, inner_kernels, last_kernel, tile_layer)
    clean = (noisy_image - SIGMA_NOW * predicted) / SCALE_NOW
    clean_wide = lax.all_gather(clean, "col", axis=2, tiled=True)
    maps_real = coil_maps[:, 0]
    maps_imag = coil_maps[:, 1]
    coil_count, row_count, full_cols = maps_real.shape
    coil_pair = complex_mul((maps_real, maps_imag), (clean_wide[0][None], clean_wide[1][None]))
    spectra = transform_last(
        (
            coil_pair[0].reshape(coil_count * row_count, full_cols),
            coil_pair[1].reshape(coil_count * row_count, full_cols),
        ),
        W_FAC,
        -1.0,
    )
    groups = lax.axis_size("gz")
    pencil = full_cols // groups
    arrived = (
        lax.all_to_all(
            spectra[0].reshape(groups, pencil, coil_count, row_count),
            "gz",
            split_axis=0,
            concat_axis=3,
            tiled=True,
        ),
        lax.all_to_all(
            spectra[1].reshape(groups, pencil, coil_count, row_count),
            "gz",
            split_axis=0,
            concat_axis=3,
            tiled=True,
        ),
    )
    item_count = arrived[0].shape[2]
    height = arrived[0].shape[3]
    flattened = (
        arrived[0].reshape(pencil * item_count, height),
        arrived[1].reshape(pencil * item_count, height),
    )
    transformed = transform_last(flattened, H_FAC, -1.0)
    keeping = sampled.astype(jnp.float32)[:, None, :]
    resid_real = keeping * (transformed[0].T.reshape(pencil, item_count, height) - measured[0])
    resid_imag = keeping * (transformed[1].T.reshape(pencil, item_count, height) - measured[1])
    height = resid_real.shape[2]
    inverse = transform_last(
        (
            resid_real.reshape(pencil * coil_count, height),
            resid_imag.reshape(pencil * coil_count, height),
        ),
        H_FAC,
        1.0,
    )
    arrived = (
        lax.all_to_all(
            inverse[0].T.reshape(pencil, coil_count, groups, row_count),
            "gz",
            split_axis=2,
            concat_axis=0,
            tiled=True,
        ),
        lax.all_to_all(
            inverse[1].T.reshape(pencil, coil_count, groups, row_count),
            "gz",
            split_axis=2,
            concat_axis=0,
            tiled=True,
        ),
    )
    item_count = arrived[0].shape[1]
    flattened = (
        arrived[0].reshape(full_cols, item_count * row_count),
        arrived[1].reshape(full_cols, item_count * row_count),
    )
    transformed = transform_first(flattened, W_FAC, 1.0)
    back_real = jnp.transpose(transformed[0].reshape(full_cols, item_count, row_count), (1, 2, 0))
    back_imag = jnp.transpose(transformed[1].reshape(full_cols, item_count, row_count), (1, 2, 0))
    grad_real = jnp.sum(maps_real * back_real + maps_imag * back_imag, axis=0)
    grad_imag = jnp.sum(maps_real * back_imag - maps_imag * back_real, axis=0)
    grad_tile = lax.psum_scatter(
        jnp.stack([grad_real, grad_imag]), "col", scatter_dimension=2, tiled=True
    )
    update = clean - STEP_GAIN * grad_tile
    return SCALE_NEXT * update + DIRECT_GAIN * predicted + NOISE_GAIN * fresh_noise


def solution(mesh):
    in_specs = (
        P("grp", "gz", "col"),
        P("grp", "gz", "col"),
        P("col", "grp", "gz", None),
        P("grp", "gz", "col", None),
        P("gz", "grp"),
        P(),
        P(),
        P(),
    )
    out_specs = P("grp", "gz", "col")
    return jax.shard_map(local, mesh=mesh, in_specs=in_specs, out_specs=out_specs, check_vma=False)
```

profile of v0, /device:TPU:0, one launch (start us, length us, event | category | flops | bytes accessed | tf_op | source)
XLA Modules:
  0.0 963.8 jit_solution(11857131419789842117)
XLA Ops:
  7.6 4.9 collective-permute-start
  13.8 4.2 collective-permute-done.1
  24.2 6.6 copy.217
  31.1 19.7 %convolution_select_fusion.1 = f32[128,8,49,64]{3,1,2,0:T(8,128)} fusion(bf16[3,3,64,2]{2,3,1,0:T(2,128)(2,1)S(1)} %bitcast.255, pred[8,49]{0,1:T(8,128)(4,1)S(1)} %copy-done.32, bf16[2,130,1,7,2]{3,0,4,1,2:T(2,128)(2,1)S(1)} %slice.81, bf16[2,130,1,8,49]{3,0,4,1,2:T(2,128)(2,1)S(1)} %copy.217), kind=kOutput, calls=%fused_computation.4 | convolution fusion | flops 119453248 | bytes 13058872 | tf_op jit(solution)/shard_map/conv_general_dilated | solution.py:38
  50.7 21.8 %copy.218 = f32[128,8,49,64]{0,3,2,1:T(8,128)} copy(f32[128,8,49,64]{3,1,2,0:T(8,128)} %convolution_select_fusion.1) | data formatting | bytes 25690112 | tf_op jit(solution)/shard_map/conv_general_dilated | solution.py:38
  72.6 6.6 multiply_convert_fusion.1
  79.2 6.5 fusion.345
  85.7 8.6 copy.219
  94.3 4.3 collective-permute-start.4
  98.7 8.6 copy.220
  108.8 9.8 %copy.221 = bf16[64,1,384]{1,0,2:T(8,128)(2,1)} copy(bf16[64,1,384]{2,0,1:T(8,128)(2,1)S(1)} %collective-permute-done.4) | data formatting | bytes 98304 | tf_op jit(solution)/shard_map/ppermute | solution.py:26
  118.6 9.8 %copy.222 = bf16[64,1,384]{1,0,2:T(8,128)(2,1)} copy(bf16[64,1,384]{2,0,1:T(8,128)(2,1)S(1)} %collective-permute-done.5) | data formatting | bytes 98304 | tf_op jit(solution)/shard_map/ppermute | solution.py:29
  134.7 13.6 %maximum_bitcast_fusion = bf16[64,130,1,386]{1,0,3,2:T(8,128)(2,1)S(1)} fusion(bf16[64,130,1]{1,0,2:T(8,128)(2,1)S(1)} %collective-permute-done.7, bf16[64,1,384]{1,0,2:T(8,128)(2,1)S(1)} %copy-done.4, bf16[64,128,384]{1,0,2:T(8,128)(2,1)S(1)} %bitcast.231, bf16[64,1,384]{1,0,2:T(8,128)(2,1)} %copy.221, bf16[64,130,1]{1,0,2:T(8,128)(2,1)S(1)} %collective-permute-done.6), kind=kLoop, calls=%fused_computation.14 | loop fusion | flops 32115200 | bytes 12846080 | tf_op jit(solution)/shard_map/broadcast_in_dim | solution.py:39
  148.4 6.7 pad.2
  155.1 23.4 %copy.224 = bf16[64,130,1,8,49]{0,3,4,1,2:T(8,128)(2,1)} copy(bf16[64,130,1,8,49]{1,0,4,3,2:T(8,128)(2,1)} %bitcast.233) | data formatting | bytes 13045760 | tf_op jit(solution)/shard_map/conv_general_dilated | solution.py:38
  179.7 35.2 %convolution_select_fusion = f32[128,8,49,64]{3,1,2,0:T(8,128)} fusion(bf16[3,3,64,64]{3,2,1,0:T(8,128)(2,1)S(1)} %bitcast.229, bf16[64,130,1,7,2]{0,3,4,1,2:T(8,128)(2,1)S(1)} %slice.85, bf16[64,130,1,8,49]{0,3,4,1,2:T(8,128)(2,1)} %copy.224, pred[8,49]{0,1:T(8,128)(4,1)S(1)} %copy-done.32), kind=kOutput, calls=%fused_computation.3 | convolution fusion | flops 3722954752 | bytes 19675016 | tf_op jit(solution)/shard_map/conv_general_dilated | solution.py:38
  214.9 22.1 %copy.225 = f32[128,8,49,64]{0,3,2,1:T(8,128)} copy(f32[128,8,49,64]{3,1,2,0:T(8,128)} %convolution_select_fusion) | data formatting | bytes 25690112 | tf_op jit(solution)/shard_map/conv_general_dilated | solution.py:38
  237.0 6.6 multiply_convert_fusion
  243.6 6.5 fusion.344
  250.1 8.6 copy.226
  258.7 4.4 collective-permute-start.8
  263.1 8.6 copy.227
  273.1 3.4 fusion.347
  276.4 9.8 %copy.228 = bf16[64,1,384]{1,0,2:T(8,128)(2,1)} copy(bf16[64,1,384]{2,0,1:T(8,128)(2,1)S(1)} %collective-permute-done.8) | data formatting | bytes 98304 | tf_op jit(solution)/shard_map/ppermute | solution.py:26
  286.2 9.8 %copy.229 = bf16[64,1,384]{1,0,2:T(8,128)(2,1)} copy(bf16[64,1,384]{2,0,1:T(8,128)(2,1)S(1)} %collective-permute-done.9) | data formatting | bytes 98304 | tf_op jit(solution)/shard_map/ppermute | solution.py:29
  306.0 13.8 %maximum_bitcast_fusion.1 = bf16[64,130,1,386]{1,0,3,2:T(8,128)(2,1)S(1)} fusion(bf16[64,130,1]{1,0,2:T(8,128)(2,1)S(1)} %collective-permute-done.11, bf16[64,1,384]{1,0,2:T(8,128)(2,1)} %copy.229, bf16[64,128,384]{1,0,2:T(8,128)(2,1)} %copy-done.2, bf16[64,1,384]{1,0,2:T(8,128)(2,1)} %copy.228, bf16[64,130,1]{1,0,2:T(8,128)(2,1)S(1)} %collective-permute-done.10), kind=kLoop, calls=%fused_computation.15 | loop fusion | flops 32115200 | bytes 12846080 | tf_op jit(solution)/shard_map/broadcast_in_dim | solution.py:39
  319.8 6.6 pad.4
  326.4 23.3 %copy.231 = bf16[64,130,1,8,49]{0,3,4,1,2:T(8,128)(2,1)} copy(bf16[64,130,1,8,49]{1,0,4,3,2:T(8,128)(2,1)} %bitcast.232) | data formatting | bytes 13045760 | tf_op jit(solution)/shard_map/conv_general_dilated | solution.py:38
  350.9 285.6 %fusion.10 = f32[128,8,49,2]{1,3,2,0:T(2,128)} fusion(bf16[3,3,2,64]{3,2,1,0:T(2,128)(2,1)S(1)} %bitcast.256, bf16[64,130,1,7,2]{0,3,4,1,2:T(8,128)(2,1)S(1)} %slice.89, bf16[64,130,1,8,49]{0,3,4,1,2:T(8,128)(2,1)} %copy.231), kind=kOutput, calls=%fused_computation.12 | convolution fusion | flops 135972864 | bytes 7159552 | tf_op jit(solution)/shard_map/conv_general_dilated | solution.py:38
  636.5 7.0 copy.232
  645.1 3.1 all_gather.3
  651.7 2.4 mul.877
  654.2 2.9 mul.878
  657.1 4.3 multiply_subtract_fusion.4
  663.5 3.2 fusion.131
  672.9 2.5 multiply_subtract_fusion.1
  681.4 2.8 mul.896
  684.2 6.9 all-to-all-start.1
  691.1 3.4 fusion.58
  699.2 29.5 %all-to-all-done.1 = f32[8,96,4,128]{3,2,1,0:T(4,128)} async-done(((f32[8,96,4,128]{3,2,1,0:T(4,128)}), f32[8,96,4,128]{3,2,1,0:T(4,128)}, u32[]{:S(2)}, u32[]{:S(2)}) %all-to-all-start.1) | async-done | bytes 1572896 | tf_op jit(solution)/shard_map/all_to_all | solution.py:160
  728.7 4.3 all-to-all-start
  734.1 3.8 fusion.346
  742.1 3.6 copy.249
  745.7 23.9 %all-to-all-done = f32[8,96,4,128]{3,2,1,0:T(4,128)} async-done(((f32[8,96,4,128]{3,2,1,0:T(4,128)}), f32[8,96,4,128]{3,2,1,0:T(4,128)}, u32[]{:S(2)}, u32[]{:S(2)}) %all-to-all-start) | async-done | bytes 1572896 | tf_op jit(solution)/shard_map/all_to_all | solution.py:153
  780.1 2.9 fusion.46
  787.3 3.0 copy.257
  790.3 3.7 subtract_multiply_fusion.4
  796.1 3.1 copy.253
  799.2 3.5 fusion.137
  815.4 3.8 all-to-all-start.3
  828.7 27.6 %all-to-all-done.3 = f32[96,4,8,128]{3,1,0,2:T(4,128)S(1)} async-done(((f32[96,4,8,128]{3,1,0,2:T(4,128)}), f32[96,4,8,128]{3,1,0,2:T(4,128)S(1)}, u32[]{:S(2)}, u32[]{:S(2)}) %all-to-all-start.3) | async-done | bytes 1572896 | tf_op jit(solution)/shard_map/all_to_all | solution.py:195
  856.3 4.3 all-to-all-start.2
  862.1 4.0 fusion.19
  866.1 4.0 fusion.17
  870.1 27.2 %all-to-all-done.2 = f32[96,4,8,128]{3,1,0,2:T(4,128)} async-done(((f32[96,4,8,128]{3,1,0,2:T(4,128)}), f32[96,4,8,128]{3,1,0,2:T(4,128)}, u32[]{:S(2)}, u32[]{:S(2)}) %all-to-all-start.2) | async-done | bytes 1572896 | tf_op jit(solution)/shard_map/all_to_all | solution.py:188
  899.4 4.6 fusion.26
  904.0 3.2 multiply_subtract_fusion
  909.7 3.6 fusion.48
  913.3 2.7 subtract_multiply_fusion
  918.3 3.0 mul.935
  921.3 3.9 add_multiply_fusion
  927.6 3.0 mul.938
  930.5 4.3 fusion.33
  938.3 16.3 %all-reduce.3.cloned.1.call-done = f32[2,128,768]{1,0,2:T(2,128)} async-done(((f32[2,128,768]{1,0,2:T(2,128)}), f32[2,128,768]{1,0,2:T(2,128)}) %all-reduce.3.cloned.1.call-update) | async-done | bytes 786448
  (182 shorter events, 113.5 us)
Async XLA Ops:
  6.5 173.1 %copy-start = (bf16[1,9,64,64]{3,2,1,0:T(8,128)(2,1)S(1)}, bf16[1,9,64,64]{3,2,1,0:T(8,128)(2,1)}, u32[]{:S(2)}) copy-start(bf16[1,9,64,64]{3,2,1,0:T(8,128)(2,1)} %param.14) | copy-start | bytes 221188
  7.6 6.2 collective-permute-start
  12.5 5.5 collective-permute-start.1
  18.1 2.6 collective-permute-start.2
  19.4 3.2 collective-permute-start.3
  24.2 6.9 copy-start.32
  24.2 6.9 copy-start.33
  79.2 6.5 copy-start.3
  94.3 14.4 %collective-permute-start.4 = (bf16[64,1,384]{2,0,1:T(8,128)(2,1)S(1)}, bf16[64,1,384]{2,0,1:T(8,128)(2,1)S(1)}, u32[]{:S(2)}, u32[]{:S(2)}) collective-permute-start(bf16[64,1,384]{2,0,1:T(8,128)(2,1)S(1)} %copy.219), channel_id=1, source_target_pairs={{0,2},{2,4},{4,6},{6,8},{8,10},{10,12},{12,14},{1,3},{3,5},{5,7},{... | collective-permute-start | bytes 147464 | tf_op jit(solution)/shard_map/ppermute | solution.py:26
  107.3 11.3 %collective-permute-start.5 = (bf16[64,1,384]{2,0,1:T(8,128)(2,1)S(1)}, bf16[64,1,384]{2,0,1:T(8,128)(2,1)S(1)}, u32[]{:S(2)}, u32[]{:S(2)}) collective-permute-start(bf16[64,1,384]{2,0,1:T(8,128)(2,1)S(1)} %copy.220), channel_id=1, source_target_pairs={{2,0},{4,2},{6,4},{8,6},{10,8},{12,10},{14,12},{3,1},{5,3},{7,5},{... | collective-permute-start | bytes 147464 | tf_op jit(solution)/shard_map/ppermute | solution.py:29
  118.6 16.1 %slice-start = ((s8[6291456]{0:T(1024)(128)(4,1)}), s8[2097152]{0:T(1024)(128)(4,1)S(1)}, s32[]{:S(2)}) async-start(s8[6291456]{0:T(1024)(128)(4,1)} %bitcast.230), calls=%async_computation.5 | async-start | bytes 4194304
  128.4 6.4 slice-start.1
  128.4 6.4 copy-start.4
  129.4 3.5 collective-permute-start.6
  131.6 3.1 collective-permute-start.7
  243.6 6.5 copy-start.2
  258.7 17.7 %collective-permute-start.8 = (bf16[64,1,384]{2,0,1:T(8,128)(2,1)S(1)}, bf16[64,1,384]{2,0,1:T(8,128)(2,1)S(1)}, u32[]{:S(2)}, u32[]{:S(2)}) collective-permute-start(bf16[64,1,384]{2,0,1:T(8,128)(2,1)S(1)} %copy.226), channel_id=1, source_target_pairs={{0,2},{2,4},{4,6},{6,8},{8,10},{10,12},{12,14},{1,3},{3,5},{5,7},{... | collective-permute-start | bytes 147464 | tf_op jit(solution)/shard_map/ppermute | solution.py:26
  271.8 14.4 %collective-permute-start.9 = (bf16[64,1,384]{2,0,1:T(8,128)(2,1)S(1)}, bf16[64,1,384]{2,0,1:T(8,128)(2,1)S(1)}, u32[]{:S(2)}, u32[]{:S(2)}) collective-permute-start(bf16[64,1,384]{2,0,1:T(8,128)(2,1)S(1)} %copy.227), channel_id=1, source_target_pairs={{2,0},{4,2},{6,4},{8,6},{10,8},{12,10},{14,12},{3,1},{5,3},{7,5},{... | collective-permute-start | bytes 147464 | tf_op jit(solution)/shard_map/ppermute | solution.py:29
  296.9 9.1 collective-permute-start.10
  298.7 7.3 collective-permute-start.11
  301.3 1.1 copy-start.7
  304.2 1.8 copy-start.9
  326.4 24.5 %copy-start.34 = (bf16[9,2,64]{2,1,0:T(2,128)(2,1)S(1)}, bf16[9,2,64]{2,1,0:T(2,128)(2,1)}, u32[]{:S(2)}) copy-start(bf16[9,2,64]{2,1,0:T(2,128)(2,1)} %param.15) | copy-start | bytes 6916
  643.5 1.3 copy-start.29
  644.9 4.7 copy-start.26
  654.2 2.9 copy-start.25
  663.4 3.2 copy-start.5
  668.9 1.9 copy-start.23
  670.8 2.1 copy-start.6
  675.3 1.8 copy-start.20
  684.2 44.5 %all-to-all-start.1 = ((f32[8,96,4,128]{3,2,1,0:T(4,128)}), f32[8,96,4,128]{3,2,1,0:T(4,128)}, u32[]{:S(2)}, u32[]{:S(2)}) async-start(f32[8,96,4,128]{3,2,1,0:T(4,128)} %mul.896), calls=%async_computation.1 | async-start | bytes 3145728 | tf_op jit(solution)/shard_map/all_to_all | solution.py:160
  699.2 33.8 %copy-start.30 = (s32[96,1024]{1,0:T(8,128)S(1)}, s32[96,1024]{1,0:T(8,128)}, u32[]{:S(2)}) copy-start(s32[96,1024]{1,0:T(8,128)} %param.12) | copy-start | bytes 1179652
  728.7 41.0 %all-to-all-start = ((f32[8,96,4,128]{3,2,1,0:T(4,128)}), f32[8,96,4,128]{3,2,1,0:T(4,128)}, u32[]{:S(2)}, u32[]{:S(2)}) async-start(f32[8,96,4,128]{3,2,1,0:T(4,128)} %mul.894), calls=%async_computation | async-start | bytes 3145728 | tf_op jit(solution)/shard_map/all_to_all | solution.py:153
  772.0 1.5 copy-start.16
  778.3 1.8 copy-start.17
  799.2 3.5 copy-start.15
  802.7 1.6 copy-start.18
  802.7 1.9 copy-start.19
  808.4 1.8 copy-start.11
  808.4 1.8 copy-start.13
  815.4 3.8 copy-start.14
  815.4 40.9 %all-to-all-start.3 = ((f32[96,4,8,128]{3,1,0,2:T(4,128)}), f32[96,4,8,128]{3,1,0,2:T(4,128)S(1)}, u32[]{:S(2)}, u32[]{:S(2)}) async-start(f32[96,4,8,128]{3,1,0,2:T(4,128)} %copy.268), calls=%async_computation.3 | async-start | bytes 3145728 | tf_op jit(solution)/shard_map/all_to_all | solution.py:195
  819.1 1.8 copy-start.12
  856.3 40.9 %all-to-all-start.2 = ((f32[96,4,8,128]{3,1,0,2:T(4,128)}), f32[96,4,8,128]{3,1,0,2:T(4,128)}, u32[]{:S(2)}, u32[]{:S(2)}) async-start(f32[96,4,8,128]{3,1,0,2:T(4,128)} %copy.262), calls=%async_computation.2 | async-start | bytes 3145728 | tf_op jit(solution)/shard_map/all_to_all | solution.py:188
  860.6 94.0 %all-reduce.3.cloned.1.call-start = ((), (), s32[]{:S(2)}) async-start(), calls=%async_computation.4 | async-start | bytes 1572864
  899.4 4.6 copy-start.24
  907.2 2.5 copy-start.21
  918.3 3.0 copy-start.22
  927.5 3.0 copy-start.8
  927.5 3.0 copy-start.10
  934.8 1.7 copy-start.35
  934.8 3.0 copy-start.28
  938.1 17.8 %copy-start.27 = (f32[2,128,384]{2,1,0:T(8,128)S(1)}, f32[2,128,384]{2,1,0:T(8,128)}, u32[]{:S(2)}) copy-start(f32[2,128,384]{2,1,0:T(8,128)} %copy-done.26) | copy-start | bytes 1179652
  938.1 17.8 %copy-start.31 = (f32[2,128,384]{2,1,0:T(8,128)S(1)}, f32[2,128,384]{2,1,0:T(8,128)}, u32[]{:S(2)}) copy-start(f32[2,128,384]{2,1,0:T(8,128)} %param.9) | copy-start | bytes 1179652
  954.6 2.1 copy-start.1
Sparse Core Ops, SparseCore 0:
  936.6 18.0 all-reduce.2
where the time goes:
time: 976 us; the launch traced here: 964 us
  matrix products  421 us (43%)
  local copies, waits for them, and re-layouts  289 us (30%)
  waiting for transfers between devices  132 us (14%)
  other arithmetic  56.3 us (6%)
  starting transfers between devices  46.5 us (5%)
  between operations  15.4 us (2%)
    conv_general_dilated x3, matrix products, convolve_padded(): lax.conv_general_dilated(padded[None], filters, (1, 1), 'VALID', dimensio...  341 us
    conv_general_dilated x10, local copies, waits for them, and re-layouts, convolve_padded(): lax.conv_general_dilated(padded[None], filters, (1, 1), 'VALID', dimensio...  108 us
    slice x5, local copies, waits for them, and re-layouts, with_halo(): lax.slice_in_dim(block, block.shape[dim] - width, None, axis=dim)  30.2 us
    all_to_all x1, waiting for transfers between devices, local(): lax.all_to_all(spectra[1].reshape(groups, pencil, coil_count, row_count),...  29.5 us
    broadcast_in_dim x3, other arithmetic, convolve_padded(): padded[None]  27.6 us
    all_to_all x1, waiting for transfers between devices, local(): lax.all_to_all(inverse[1].T.reshape(pencil, coil_count, groups, row_count...  27.6 us
    all_to_all x1, waiting for transfers between devices, local(): lax.all_to_all(inverse[0].T.reshape(pencil, coil_count, groups, row_count...  27.2 us
    all_to_all x1, waiting for transfers between devices, local(): lax.all_to_all(spectra[0].reshape(groups, pencil, coil_count, row_count),...  23.9 us
  transfers between devices with their start and end apart: 17, of which 8 were waited for; matrix products, arithmetic and copies ran while one was open for 9% of the time, Pallas kernels for 0%

commit v1 on v0

v1 whole, which is shorter than its diff:
```python
import math

import jax
import jax.numpy as jnp
import ml_dtypes
import numpy as np
from jax import lax
from jax.experimental import pallas as pl
from jax.experimental.pallas import tpu as pltpu
from jax.sharding import PartitionSpec as P

SCALE_NOW = 0.8
SIGMA_NOW = 0.6
STEP_GAIN = 1.0
SCALE_NEXT = 0.9
DIRECT_GAIN = 0.31622776601683794
NOISE_GAIN = 0.3

NOISY_MAX = 6.0
MAPS_MAX = 1.5
MEASURED_MAX = 2.4

F32 = jnp.float32
BF16 = jnp.bfloat16
LANES = 128
EDGE = 8


def ceil_to(value, step):
    return -(-value // step) * step


def tap_choice(rows, cols):
    choice = np.zeros(rows.shape + (9,), np.float32)
    for index in np.ndindex(rows.shape):
        a, b = rows[index], cols[index]
        if 0 <= a < 3 and 0 <= b < 3:
            choice[index + (3 * a + b,)] = 1.0
    return choice


def pick_taps(choice, kernel):
    flat = lax.dot_general(
        jnp.asarray(choice.reshape(-1, 9), BF16),
        kernel.reshape(9, -1),
        (((1,), (0,)), ((), ())),
        preferred_element_type=F32,
    ).astype(BF16)
    return flat.reshape(choice.shape[:-1] + kernel.shape[1:])


def network_weights(first_kernel, inner_kernel, last_kernel):
    s, d, x, c, r = np.meshgrid(*map(np.arange, (4, 4, 16, 2, 2)), indexing="ij")
    first = pick_taps(tap_choice(x - 5 - 2 * s - r, d - c), first_kernel * jnp.asarray(0.5, BF16))
    first = jnp.transpose(first, (0, 1, 6, 2, 3, 4, 5)).reshape(4, 128, -1)
    places = []
    for cols, rows in (((0, 1), (0, 1)), ((-1, 2), (0, 1)), ((0, 1), (2, -1)), ((-1, 2), (2, -1))):
        places += [(gamma, rho) for gamma in cols for rho in rows]
    gamma = np.array([p[0] for p in places])[:, None, None]
    rho = np.array([p[1] for p in places])[:, None, None]
    c, r = np.arange(2)[None, :, None], np.arange(2)[None, None, :]
    rows, cols = np.broadcast_arrays(rho - r + 1, gamma - c + 1)
    inner = pick_taps(tap_choice(rows, cols), inner_kernel * jnp.asarray(0.5, BF16))
    ch = inner_kernel.shape[1]
    inner = jnp.transpose(inner, (0, 4, 1, 2, 3)).reshape(16 * ch, 4 * ch)
    dr, dc, c, r = np.meshgrid(*map(np.arange, (4, 4, 2, 2)), indexing="ij")
    last = pick_taps(tap_choice(r - dr + 2, c - dc + 2), last_kernel)
    last = jnp.transpose(last, (0, 1, 4, 2, 3, 5)).reshape(32, -1)
    return first, inner, last


def split3(value):
    high = value.astype(BF16)
    rest = value - high.astype(F32)
    middle = rest.astype(BF16)
    return high, middle, (rest - middle.astype(F32)).astype(BF16)


def split2(value):
    high = value.astype(BF16)
    return high, (value - high.astype(F32)).astype(BF16)


def mm(lhs, rhs):
    return lax.dot_general(lhs, rhs, (((1,), (0,)), ((), ())), preferred_element_type=F32)


def mm_nt(lhs, rhs):
    return lax.dot_general(lhs, rhs, (((1,), (1,)), ((), ())), preferred_element_type=F32)


def network_kernel(
    flags, top, center, bottom, side, first, inner, last, pred, clean, tile, q, hid, hid_side, mask, acc
):
    rows, cols = center.shape[1:]
    blocks = rows // 2 + 2
    groups = q.shape[1] // 8 - 1
    used = mask.shape[0]

    for ch in range(2):
        tile[ch, 0:8, :] = top[ch]
        tile[ch, 8 : 8 + rows, :] = center[ch]
        tile[ch, 8 + rows : 16 + rows, :] = bottom[ch]
    w = lax.broadcasted_iota(jnp.int32, (cols, 256), 0)
    k = lax.broadcasted_iota(jnp.int32, (cols, 256), 1)
    e = lax.broadcasted_iota(jnp.int32, (2 * EDGE, 256), 0)
    e = jnp.where(e < EDGE, e - EDGE, e - EDGE + cols)
    ke = lax.broadcasted_iota(jnp.int32, (2 * EDGE, 256), 1)
    for d in range(4):
        sel = jnp.where(w == 2 * k - 3 + d, 1.0, 0.0).astype(BF16)
        sel_side = jnp.where(e == 2 * ke - 3 + d, 1.0, 0.0).astype(BF16)
        for ch in range(2):
            q[2 * d + ch] = mm(tile[ch].astype(BF16), sel) + mm(side[ch].astype(BF16), sel_side)

    ks = lax.broadcasted_iota(jnp.int32, (used, 256), 0)
    drop_low = jnp.where(flags[2] != 0, 0, -1)
    drop_high = jnp.where(flags[3] != 0, cols // 2 + 1, -1)
    mask[...] = jnp.where((ks == drop_low) | (ks == drop_high), 0.0, 1.0)
    acc[...] = jnp.zeros(acc.shape, F32)

    def first_layer(t, carry):
        window = q[:, pl.ds(pl.multiple_of(8 * t, 8), 16), :].reshape(128, 256)
        window = jnp.transpose(window)[:used].astype(BF16)
        for s in range(4):
            half = mm(window, first[s])
            h = (half + half * jnp.tanh(half)) * mask[...]
            hid[4 * t + s] = h.astype(BF16)
            hid_side[4 * t + s, :, 0:128] = pltpu.roll(h[:, 128:256], 1, 0).astype(BF16)
            hid_side[4 * t + s, :, 128:256] = pltpu.roll(h[:, 0:128], used - 1, 0).astype(BF16)
        return carry

    lax.fori_loop(0, groups, first_layer, 0)

    for flag, j in ((0, 0), (1, blocks - 1)):

        @pl.when(flags[flag] != 0)
        def _(j=j):
            hid[j] = jnp.zeros(hid.shape[1:], BF16)
            hid_side[j] = jnp.zeros(hid_side.shape[1:], BF16)

    lane = lax.broadcasted_iota(jnp.int32, (used, 256), 1)
    below = lax.rem(lane, 128) < 64

    def next_layers(j, carry):
        up, down = jnp.maximum(j - 1, 0), j + 1
        half = mm(hid[j], inner[0:256, :]) + mm(hid_side[j], inner[256:512, :])
        half += mm(jnp.where(below, hid[down], hid[up]), inner[512:768, :])
        half += mm(jnp.where(below, hid_side[down], hid_side[up]), inner[768:1024, :])
        h = ((half + half * jnp.tanh(half)) * mask[...]).astype(BF16)
        part = mm_nt(last[...], h)
        gone = ((j == 0) & (flags[0] != 0)) | ((j == blocks - 1) & (flags[1] != 0))
        part = part * jnp.where(gone, 0.0, 1.0)
        where = pl.ds(pl.multiple_of(16 * j, 16), 32)
        for c in range(0, used, 128):
            width = min(128, used - c)
            acc[c // 128, where, 0:width] = acc[c // 128, where, 0:width] + part[:, c : c + width]
        return carry

    lax.fori_loop(0, blocks, next_layers, 0)

    k = lax.broadcasted_iota(jnp.int32, (256, cols), 0)
    w = lax.broadcasted_iota(jnp.int32, (256, cols), 1)
    total = [0.0, 0.0]
    for d in range(4):
        sel = jnp.where(w == 2 * k - 3 + d, 1.0, 0.0).astype(BF16)
        for ch in range(2):
            start = 24 + 2 * d + ch
            lines = jnp.concatenate(
                [acc[c, pl.ds(start, rows, stride=8), :] for c in range(2)], axis=1
            )
            for piece in split3(lines):
                total[ch] += mm(piece, sel)
    for ch in range(2):
        pred[ch] = total[ch]
        clean[ch] = (center[ch] - SIGMA_NOW * total[ch]) / SCALE_NOW


def run_network(noisy, top, bottom, side, flags, weights):
    _, rows, cols = noisy.shape
    blocks = rows // 2 + 2
    groups = -(-blocks // 4)
    used = ceil_to(cols // 2 + 2, 16)
    vmem = pl.BlockSpec(memory_space=pltpu.VMEM)
    shape = jax.ShapeDtypeStruct(noisy.shape, F32)
    return pl.pallas_call(
        network_kernel,
        out_shape=(shape, shape),
        in_specs=[pl.BlockSpec(memory_space=pltpu.SMEM)] + [vmem] * 7,
        out_specs=(vmem, vmem),
        scratch_shapes=[
            pltpu.VMEM((2, rows + 16, cols), F32),
            pltpu.VMEM((8, 8 * groups + 8, 256), F32),
            pltpu.VMEM((4 * groups, used, 256), BF16),
            pltpu.VMEM((4 * groups, used, 256), BF16),
            pltpu.VMEM((used, 256), F32),
            pltpu.VMEM((2, 16 * blocks + 16, 128), F32),
        ],
        name="network",
    )(flags, top, noisy, bottom, side, *weights)


def move(value, axis, pairs):
    return lax.ppermute(value, axis, pairs)


def halo(noisy):
    gz, col = lax.axis_size("gz"), lax.axis_size("col")
    _, rows, cols = noisy.shape
    upper, lower = noisy[:, :EDGE, :], noisy[:, rows - EDGE :, :]
    left, right = noisy[:, :, :EDGE], noisy[:, :, cols - EDGE :]
    down = [(i, i + 1) for i in range(gz - 1)]
    top = move(lower, "gz", down)
    bottom = move(upper, "gz", [(b, a) for a, b in down])

    def both(dr, dc):
        return [
            (r * col + c, (r + dr) * col + c + dc)
            for r in range(gz)
            for c in range(col)
            if 0 <= r + dr < gz and 0 <= c + dc < col
        ]

    def side(dc, edge):
        parts = [
            move(edge[:, rows - EDGE :], ("gz", "col"), both(1, dc)),
            move(edge, "col", [(c, c + dc) for c in range(col) if 0 <= c + dc < col]),
            move(edge[:, :EDGE], ("gz", "col"), both(-1, dc)),
        ]
        return parts

    if col == 2:
        first = lax.axis_index("col") == 0
        edge = jnp.where(first, right, left)
        swap = [(0, 1), (1, 0)]

        def cross(dr):
            return [
                (r * 2 + c, (r + dr) * 2 + 1 - c)
                for r in range(gz)
                for c in range(2)
                if 0 <= r + dr < gz
            ]

        got = jnp.concatenate(
            [
                move(edge[:, rows - EDGE :], ("gz", "col"), cross(1)),
                move(edge, "col", swap),
                move(edge[:, :EDGE], ("gz", "col"), cross(-1)),
            ],
            axis=1,
        )
        zero = jnp.zeros_like(got)
        sides = jnp.concatenate(
            [jnp.where(first, zero, got), jnp.where(first, got, zero)], axis=2
        )
    else:
        sides = jnp.concatenate(
            [
                jnp.concatenate(side(1, right), axis=1),
                jnp.concatenate(side(-1, left), axis=1),
            ],
            axis=2,
        )
    return top, bottom, sides


def edge_flags():
    row, col = lax.axis_index("gz"), lax.axis_index("col")
    last_row, last_col = lax.axis_size("gz") - 1, lax.axis_size("col") - 1
    return jnp.stack([row == 0, row == last_row, col == 0, col == last_col]).astype(jnp.int32)


def halves(matrix):
    high = matrix.astype(ml_dtypes.bfloat16)
    low = (matrix - high.astype(np.float64)).astype(ml_dtypes.bfloat16)
    return np.stack([high, low])


def fourier_parts(length, scale):
    index = np.arange(length)
    angle = 2.0 * np.pi * (np.outer(index, index) % length) / length
    return np.cos(angle) * scale, np.sin(angle) * scale


def turn_table(radix, inner):
    angle = 2.0 * np.pi * np.outer(np.arange(radix), np.arange(inner)) / (radix * inner)
    return np.stack([np.cos(angle), np.sin(angle)]).astype(np.float32)


def small_dft(values, sign):
    n = len(values)
    if n == 1:
        return values
    if n % 2 == 0:
        even = small_dft(values[0::2], sign)
        odd = small_dft(values[1::2], sign)
        low, high = [], []
        for q in range(n // 2):
            re, im = times_unit(odd[q], q, n, sign)
            low.append((even[q][0] + re, even[q][1] + im))
            high.append((even[q][0] - re, even[q][1] - im))
        return low + high
    if n == 3:
        (r0, i0), (r1, i1), (r2, i2) = values
        sr, si = r1 + r2, i1 + i2
        half = math.sqrt(3.0) / 2.0 * sign
        dr, di = half * (r1 - r2), half * (i1 - i2)
        tr, ti = r0 - 0.5 * sr, i0 - 0.5 * si
        return [(r0 + sr, i0 + si), (tr - di, ti + dr), (tr + di, ti - dr)]
    out = []
    for q in range(n):
        terms = [times_unit(v, a * q, n, sign) for a, v in enumerate(values)]
        out.append((sum(t[0] for t in terms), sum(t[1] for t in terms)))
    return out


def times_unit(value, power, n, sign):
    re, im = value
    power %= n
    if power == 0:
        return re, im
    if 4 * power == n:
        return (-im, re) if sign > 0 else (im, -re)
    if 2 * power == n:
        return -re, -im
    if 4 * power == 3 * n:
        return (im, -re) if sign > 0 else (-im, re)
    c = math.cos(2.0 * math.pi * power / n)
    s = sign * math.sin(2.0 * math.pi * power / n)
    return c * re - s * im, c * im + s * re


def turn(value, cos, sin, sign):
    re, im = value
    if sign > 0:
        return re * cos - im * sin, im * cos + re * sin
    return re * cos + im * sin, im * cos - re * sin


def mm3(lhs, rhs, dot):
    return dot(lhs[0], rhs[0]) + (dot(lhs[0], rhs[1]) + dot(lhs[1], rhs[0]))


def columns_forward_kernel(first, mine, other, maps, matrix, table, out):
    radix, inner = table.shape[1:]
    rows, cols = mine.shape[1:]
    groups = out.shape[0]
    per = inner // groups
    lead = first[0] != 0
    image = [
        jnp.concatenate(
            [jnp.where(lead, mine[p], other[p]), jnp.where(lead, other[p], mine[p])], axis=1
        )
        for p in range(2)
    ]
    maps_real, maps_imag = maps[0, 0], maps[0, 1]
    coil = (
        maps_real * image[0] - maps_imag * image[1],
        maps_real * image[1] + maps_imag * image[0],
    )
    parts = [
        tuple(v[:, a * inner : (a + 1) * inner] for v in coil) for a in range(radix)
    ]
    for q, part in enumerate(small_dft(parts, -1)):
        if q:
            part = turn(part, table[0, q : q + 1, :], table[1, q : q + 1, :], -1)
        data = split2(jnp.concatenate(part, axis=1))
        result = mm3((matrix[0], matrix[1]), data, mm_nt)
        for p in range(2):
            for g in range(groups):
                start = p * inner + g * per
                out[g, p, 0, q] = result[start : start + per]


def columns_forward(mine, other, maps, groups):
    coils, _, rows, cols = maps.shape
    inner = 256
    radix = cols // inner
    c, s = fourier_parts(inner, 1.0 / math.sqrt(cols))
    matrix = halves(np.block([[c, s], [-s, c]]))
    table = turn_table(radix, inner)
    first = (lax.axis_index("col") == 0).astype(jnp.int32)[None]
    vmem = pl.BlockSpec(memory_space=pltpu.VMEM)
    per = inner // groups
    return pl.pallas_call(
        columns_forward_kernel,
        out_shape=jax.ShapeDtypeStruct((groups, 2, coils, radix, per, rows), F32),
        grid=(coils,),
        in_specs=[
            pl.BlockSpec(memory_space=pltpu.SMEM),
            vmem,
            vmem,
            pl.BlockSpec((1, 2, rows, cols), lambda i: (i, 0, 0, 0)),
            vmem,
            vmem,
        ],
        out_specs=pl.BlockSpec(
            (groups, 2, 1, radix, per, rows), lambda i: (0, 0, i, 0, 0, 0)
        ),
        name="columns_forward",
    )(first, mine, other, maps, jnp.asarray(matrix), jnp.asarray(table))


def rows_kernel(data, kept, target, forward, inverse, table, out):
    radix = table.shape[1]
    parts = small_dft([(data[a, 0], data[a, 1]) for a in range(radix)], -1)
    back = []
    for q, part in enumerate(parts):
        cos, sin = table[0, q : q + 1, :], table[1, q : q + 1, :]
        if q:
            part = turn(part, cos, sin, -1)
        spectrum = mm3(split2(jnp.concatenate(part, axis=1)), (forward[0], forward[1]), mm)
        keep = kept[q]
        residual = jnp.concatenate(
            [
                keep * (spectrum[:, p * LANES : (p + 1) * LANES] - target[p, q])
                for p in range(2)
            ],
            axis=1,
        )
        lines = mm3(split2(residual), (inverse[0], inverse[1]), mm)
        part = (lines[:, :LANES], lines[:, LANES:])
        if q:
            part = turn(part, cos, sin, 1)
        back.append(part)
    for a, (re, im) in enumerate(small_dft(back, 1)):
        out[a, 0] = re
        out[a, 1] = im


def rows_both_ways(data, kept, target):
    radix, _, count, _ = data.shape
    c, s = fourier_parts(LANES, 1.0 / math.sqrt(radix * LANES))
    forward = halves(np.block([[c, -s], [s, c]]))
    inverse = halves(np.block([[c, s], [-s, c]]))
    table = turn_table(radix, LANES)
    block = 48 if count % 48 == 0 else 8
    vmem = pl.BlockSpec(memory_space=pltpu.VMEM)
    spec = pl.BlockSpec((radix, 2, block, LANES), lambda i: (0, 0, i, 0))
    return pl.pallas_call(
        rows_kernel,
        out_shape=jax.ShapeDtypeStruct(data.shape, F32),
        grid=(count // block,),
        in_specs=[
            spec,
            pl.BlockSpec((radix, block, LANES), lambda i: (0, i, 0)),
            pl.BlockSpec((2, radix, block, LANES), lambda i: (0, 0, i, 0)),
            vmem,
            vmem,
            vmem,
        ],
        out_specs=spec,
        name="rows_both_ways",
    )(data, kept, target, jnp.asarray(forward), jnp.asarray(inverse), jnp.asarray(table))


def columns_inverse_kernel(data, maps, matrix, table, out):
    radix, inner = table.shape[1:]
    groups = data.shape[0]
    rows = out.shape[1]
    parts = []
    for q in range(radix):
        lines = jnp.concatenate(
            [data[g, p, 0, q] for p in range(2) for g in range(groups)], axis=0
        )
        lines = split2(jnp.transpose(lines))
        result = mm3(lines, (matrix[0], matrix[1]), mm)
        part = (result[:, :inner], result[:, inner:])
        if q:
            part = turn(part, table[0, q : q + 1, :], table[1, q : q + 1, :], 1)
        parts.append(part)
    back = small_dft(parts, 1)
    step = pl.program_id(0)
    for a, (re, im) in enumerate(back):
        where = slice(a * inner, (a + 1) * inner)
        maps_real, maps_imag = maps[0, 0, :, where], maps[0, 1, :, where]
        sums = (
            maps_real * re + maps_imag * im,
            maps_real * im - maps_imag * re,
        )
        for p in range(2):

            @pl.when(step == 0)
            def _(p=p, sums=sums, where=where):
                out[p, :, where] = sums[p]

            @pl.when(step != 0)
            def _(p=p, sums=sums, where=where):
                out[p, :, where] = out[p, :, where] + sums[p]


def columns_inverse(data, maps):
    groups, _, coils, radix, per, rows = data.shape
    cols = maps.shape[3]
    inner = cols // radix
    c, s = fourier_parts(inner, 1.0 / math.sqrt(cols))
    matrix = halves(np.block([[c, s], [-s, c]]))
    table = turn_table(radix, inner)
    vmem = pl.BlockSpec(memory_space=pltpu.VMEM)
    return pl.pallas_call(
        columns_inverse_kernel,
        out_shape=jax.ShapeDtypeStruct((2, rows, cols), F32),
        grid=(coils,),
        in_specs=[
            pl.BlockSpec((groups, 2, 1, radix, per, rows), lambda i: (0, 0, i, 0, 0, 0)),
            pl.BlockSpec((1, 2, rows, cols), lambda i: (i, 0, 0, 0)),
            vmem,
            vmem,
        ],
        out_specs=pl.BlockSpec((2, rows, cols), lambda i: (0, 0, 0)),
        name="columns_inverse",
    )(data, maps, jnp.asarray(matrix), jnp.asarray(table))


def send_bounds(first_kernel, inner_kernel, last_kernel, cols, height):
    def gain(kernel):
        return jnp.max(jnp.sum(jnp.abs(kernel.astype(F32)), axis=(0, 2))) * 1.02

    predicted = NOISY_MAX * gain(first_kernel) * gain(inner_kernel) * gain(last_kernel)
    clean = (NOISY_MAX + SIGMA_NOW * predicted) / SCALE_NOW
    spectra = 1.1 * math.sqrt(cols) * 2.0 * MAPS_MAX * clean
    lines = 1.1 * math.sqrt(height) * (spectra + math.sqrt(2.0) * MEASURED_MAX)
    return spectra, lines


def exchange(value, bound):
    half = (value * (60000.0 / bound)).astype(jnp.float16)
    half = lax.all_to_all(half, "gz", split_axis=0, concat_axis=0, tiled=True)
    return half.astype(F32) * (bound / 60000.0)


def local(
    noisy_image, fresh_noise, coil_maps, measured, sampled, first_kernel, inner_kernels, last_kernel
):
    groups = lax.axis_size("gz")
    coils, _, rows, cols = coil_maps.shape
    height = measured.shape[3]
    radix, inner = cols // 256, 256
    per = inner // groups
    row_radix = height // LANES

    weights = network_weights(first_kernel, inner_kernels[0], last_kernel)
    top, bottom, side = halo(noisy_image)
    predicted, clean = run_network(noisy_image, top, bottom, side, edge_flags(), weights)
    other = lax.ppermute(clean, "col", [(0, 1), (1, 0)])

    spectra_bound, lines_bound = send_bounds(
        first_kernel, inner_kernels[0], last_kernel, cols, height
    )
    spectra = columns_forward(clean, other, coil_maps, groups)
    spectra = spectra.reshape(groups, 2, coils * radix * per, rows)
    arrived = exchange(spectra, spectra_bound)
    if rows != LANES:
        arrived = jnp.transpose(arrived, (1, 2, 0, 3)).reshape(2, -1, row_radix, LANES)
        arrived = jnp.transpose(arrived, (2, 0, 1, 3))
    target = measured.reshape(2, per, radix, coils, LANES, row_radix)
    target = jnp.transpose(target, (0, 5, 3, 2, 1, 4)).reshape(2, row_radix, -1, LANES)
    kept = sampled.reshape(per, radix, LANES, row_radix).astype(F32)
    kept = jnp.transpose(kept, (3, 1, 0, 2))[:, None]
    kept = jnp.broadcast_to(kept, (row_radix, coils, radix, per, LANES))
    kept = kept.reshape(row_radix, -1, LANES)
    lines = rows_both_ways(arrived, kept, target)
    if rows != LANES:
        lines = jnp.transpose(lines, (1, 2, 0, 3)).reshape(2, -1, groups, rows)
        lines = jnp.transpose(lines, (2, 0, 1, 3))
    lines = exchange(lines, lines_bound)
    lines = lines.reshape(groups, 2, coils, radix, per, rows)
    gradient = columns_inverse(lines, coil_maps)

    first = lax.axis_index("col") == 0
    width = noisy_image.shape[2]
    own = jnp.where(first, gradient[:, :, :width], gradient[:, :, width:])
    away = jnp.where(first, gradient[:, :, width:], gradient[:, :, :width])
    own = own + lax.ppermute(away, "col", [(0, 1), (1, 0)])
    update = clean - STEP_GAIN * own
    return SCALE_NEXT * update + DIRECT_GAIN * predicted + NOISE_GAIN * fresh_noise


def solution(mesh):
    in_specs = (
        P("grp", "gz", "col"),
        P("grp", "gz", "col"),
        P("col", "grp", "gz", None),
        P("grp", "gz", "col", None),
        P("gz", "grp"),
        P(),
        P(),
        P(),
    )
    out_specs = P("grp", "gz", "col")
    return jax.shard_map(local, mesh=mesh, in_specs=in_specs, out_specs=out_specs, check_vma=False)
```

time: 976 us -> 297 us (0.30); the launches traced: 964 us -> 295 us
  matrix products: 421 us -> 3 us
  local copies, waits for them, and re-layouts: 289 us -> 138 us
  waiting for transfers between devices: 132 us -> 38.8 us
  Pallas kernels: 0 us -> 67.8 us
  other arithmetic: 56.3 us -> 19.8 us
  starting transfers between devices: 46.5 us -> 25.7 us
  between operations: 15.4 us -> 2.26 us
    conv_general_dilated x3 -> x0, matrix products: 341 us -> none  [convolve_padded(): lax.conv_general_dilated(padded[None], filters, (1, 1), 'VALID', dimensio...]
    conv_general_dilated x10 -> x0, local copies, waits for them, and re-layouts: 108 us -> none  [convolve_padded(): lax.conv_general_dilated(padded[None], filters, (1, 1), 'VALID', dimensio...]
    dot_general x32 -> x3, matrix products: 80.1 us -> 3 us  [pick_taps(): lax.dot_general(jnp.asarray(choice.reshape(-1, 9), BF16), kernel.reshape(...]
    all_to_all x4 -> x2, waiting for transfers between devices: 108 us -> 37.1 us  [exchange(): half = lax.all_to_all(half, 'gz', split_axis=0, concat_axis=0, tiled=True)]
    pallas_call x0 -> x4, Pallas kernels: none -> 67.8 us  [the longest x1 39.3 us: run_network(): pl.pallas_call(network_kernel, out_shape=(shape, shape), in_specs=[pl.Blo...]
    reshape x4 -> x10, local copies, waits for them, and re-layouts: 9.3 us -> 74.1 us  [the longest x5 39.2 us: pick_taps(): return flat.reshape(choice.shape[:-1] + kernel.shape[1:])]
    slice x10 -> x3, local copies, waits for them, and re-layouts: 56 us -> 1.89 us  [the longest x1 1.06 us: halo(): left, right = (noisy[:, :, :EDGE], noisy[:, :, cols - EDGE:])]
    transpose x2 -> x3, local copies, waits for them, and re-layouts: 2.09 us -> 48.8 us  [the longest x1 29.7 us: local(): jnp.transpose(target, (0, 5, 3, 2, 1, 4)).reshape(2, row_radix, -1, LANES)]
  transfers between devices with their start and end apart: 17 -> 9, of which waited for: 8 -> 2; matrix products, arithmetic and copies ran while one was open for 9% -> 48% of each run, Pallas kernels for 0% -> 0%
where the time goes in v1:
time: 297 us; the launch traced here: 295 us
  local copies, waits for them, and re-layouts  138 us (46%)
  Pallas kernels  67.8 us (23%)
  waiting for transfers between devices  38.8 us (13%)
  starting transfers between devices  25.7 us (9%)
  other arithmetic  19.8 us (7%)
  matrix products  3 us (1%)
    pallas_call x1, Pallas kernels, run_network(): pl.pallas_call(network_kernel, out_shape=(shape, shape), in_specs=[pl.Blo...  39.3 us
    reshape x5, local copies, waits for them, and re-layouts, pick_taps(): return flat.reshape(choice.shape[:-1] + kernel.shape[1:])  39.2 us
    all_to_all x2, waiting for transfers between devices, exchange(): half = lax.all_to_all(half, 'gz', split_axis=0, concat_axis=0, tiled=True)  37.1 us
    reshape x1, local copies, waits for them, and re-layouts, local(): target = measured.reshape(2, per, radix, coils, LANES, row_radix)  30.9 us
    transpose x1, local copies, waits for them, and re-layouts, local(): jnp.transpose(target, (0, 5, 3, 2, 1, 4)).reshape(2, row_radix, -1, LANES)  29.7 us
    transpose x1, local copies, waits for them, and re-layouts, network_weights(): first = jnp.transpose(first, (0, 1, 6, 2, 3, 4, 5)).reshape(4, 128, -1)  14.7 us
    all_to_all x2, starting transfers between devices, exchange(): half = lax.all_to_all(half, 'gz', split_axis=0, concat_axis=0, tiled=True)  13.6 us
    pallas_call x1, Pallas kernels, rows_both_ways(): pl.pallas_call(rows_kernel, out_shape=jax.ShapeDtypeStruct(data.shape, F3...  12.2 us
  transfers between devices with their start and end apart: 9, of which 2 were waited for; matrix products, arithmetic and copies ran while one was open for 48% of the time, Pallas kernels for 0%

profile of v1, /device:TPU:0, one launch (start us, length us, event | category | flops | bytes accessed | tf_op | source)
XLA Modules:
  0.0 295.4 jit_solution(12459124468255375472)
XLA Ops:
  0.0 1.1 fusion.2
  1.1 0.1 copy.43
  1.1 0.1 copy.44
  1.2 0.5 collective-permute-start.3
  1.8 0.1 fusion.4
  1.8 4.5 %collective-permute-start.2 = (f32[2,8,8]{1,2,0:T(8,128)S(1)}, f32[2,8,8]{1,2,0:T(8,128)S(1)}, u32[]{:S(2)}, u32[]{:S(2)}) collective-permute-start(f32[2,8,8]{1,2,0:T(8,128)S(1)} %get-tuple-element.15), channel_id=1, source_target_pairs={{0,3},{1,2},{2,5},{3,4},{4,7},{5,6},{6,9},{7,8},{8,11},{9,10},{10,... | collective-permute-start | bytes 1544 | tf_op jit(solution)/shard_map/ppermute | solution.py:203
  6.3 1.3 collective-permute-start.4
  7.6 0.8 fusion.3
  8.4 4.2 %collective-permute-start = (f32[2,8,384]{2,1,0:T(8,128)S(1)}, f32[2,8,384]{2,1,0:T(8,128)S(1)}, u32[]{:S(2)}, u32[]{:S(2)}) collective-permute-start(f32[2,8,384]{2,1,0:T(8,128)S(1)} %get-tuple-element.12), channel_id=1, source_target_pairs={{0,2},{2,4},{4,6},{6,8},{8,10},{10,12},{12,14},{1,3},{3,5},{5,7},{... | collective-permute-start | bytes 73736 | tf_op jit(solution)/shard_map/ppermute | solution.py:203
  12.6 1.3 collective-permute-start.1
  13.9 0.7 broadcast_multiply_fusion.1
  14.6 0.1 copy.34
  14.7 0.9 broadcast_multiply_fusion
  15.6 0.2 mul.73
  15.8 0.8 reshape.54
  16.6 1.2 fusion.1
  17.8 1.0 fusion
  18.8 0.8 convolution_convert_fusion.2
  19.6 0.6 add_convert_fusion.flags
  20.2 0.2 copy.35
  20.3 37.1 %reshape.50 = bf16[4,4,16,2,2,64,2]{6,5,4,3,2,1,0:T(8,128)(2,1)} reshape(bf16[1024,128]{1,0:T(8,128)(2,1)S(1)} %copy.35) | data formatting | bytes 524288 | tf_op jit(solution)/shard_map/reshape | solution.py:49
  57.5 14.7 %copy.36 = bf16[4,4,2,16,2,2,64]{6,5,4,3,2,1,0:T(2,128)(2,1)S(1)} copy(bf16[4,4,2,16,2,2,64]{2,6,5,4,3,1,0:T(8,128)(2,1)} %bitcast.33) | data formatting | bytes 524288 | tf_op jit(solution)/shard_map/transpose | solution.py:55
  72.2 1.1 reshape.51.first
  73.2 1.1 reshape.52
  74.3 0.0 copy-start.8
  74.4 0.0 copy-start.1
  74.4 0.0 copy-start.9
  74.4 0.8 copy.37
  75.2 1.5 reshape.53.inner
  76.7 0.1 reshape.55
  76.8 0.7 reshape.56.last
  77.5 0.0 collective-permute-done.4
  77.5 0.1 broadcast_select_fusion.1
  77.6 0.8 copy.39.side
  78.4 0.6 copy-done.6
  79.0 0.6 copy-done.7
  79.6 39.3 %network.1 = (f32[2,128,384]{2,1,0:T(8,128)}, f32[2,128,384]{2,1,0:T(8,128)}) custom-call(s32[4]{0:T(128)} %add_convert_fusion.flags, f32[2,8,384]{2,1,0:T(8,128)} %copy-done.6, f32[2,128,384]{2,1,0:T(8,128)} %center.1, f32[2,8,384]{2,1,0:T(8,128)} %copy-done.7, f32[2,144,16]{2,1,0:T(8,128)} %copy.39.side, bf16[4,128,256]{2,1,0:T(8,128)(2,1)} %reshape.51.first, ...), custom_call_target="tpu_custom_call" | custom-call | tf_op jit(solution)/shard_map/network/pallas_call | solution.py:185
  118.9 0.2 collective-permute-start.5
  119.2 0.7 reduce_max.27
  119.8 0.1 abs_reduce_fusion
  120.0 0.7 reduce_max.28
  120.6 0.1 abs_reduce_fusion.1
  120.7 0.6 reduce_max.29
  123.4 0.7 copy-done.2
  124.1 8.8 %columns_forward.1 = f32[8,2,4,3,32,128]{5,4,3,2,1,0:T(8,128)} custom-call(s32[1]{0:T(128)S(6)} %broadcast_in_dim.13.first, f32[2,128,384]{2,1,0:T(8,128)} %get-tuple-element.7.mine, f32[2,128,384]{2,1,0:T(8,128)} %copy-done.2, f32[4,2,128,768]{3,2,1,0:T(8,128)} %maps.3, bf16[2,512,512]{2,1,0:T(8,128)(2,1)} %constant.73.clone.matrix, ...), custom_call_target="tpu_custom_call" | custom-call | tf_op jit(solution)/shard_map/columns_forward/pallas_call | solution.py:385
  132.9 3.4 %multiply_convert_fusion.1 = f16[8,2,4,3,32,128]{5,4,3,2,1,0:T(8,128)(2,1)} fusion(f32[8,2,4,3,32,128]{5,4,3,2,1,0:T(8,128)} %columns_forward.1, f32[]{:T(128)S(6)} %div.13), kind=kLoop, calls=%fused_computation.5 | loop fusion | flops 1572864 | bytes 4718596 | tf_op jit(solution)/shard_map/convert_element_type | solution.py:527
  136.4 7.6 %all-to-all-start = ((f16[8,2,384,128]{3,2,1,0:T(8,128)(2,1)}), f16[8,2,384,128]{3,2,1,0:T(8,128)(2,1)}, u32[]{:S(2)}, u32[]{:S(2)}) async-start(f16[8,2,384,128]{3,2,1,0:T(8,128)(2,1)} %bitcast.10), calls=%async_computation | async-start | bytes 3145728 | tf_op jit(solution)/shard_map/all_to_all | solution.py:528
  144.0 3.7 %copy.41 = f32[2,96,4,1024]{3,1,2,0:T(8,128)S(1)} copy(f32[2,96,4,1024]{3,2,1,0:T(4,128)} %param.21) | data formatting | bytes 6291456 | tf_op args[3]
  147.7 30.9 %reshape.58 = f32[2,32,3,4,128,8]{5,4,2,1,3,0:T(8,128)} reshape(f32[2,96,4,1024]{3,1,2,0:T(8,128)S(1)} %copy.41) | data formatting | bytes 6291456 | tf_op jit(solution)/shard_map/reshape | solution.py:556
  178.6 29.7 %copy.42 = f32[2,8,4,3,32,128]{5,4,3,2,1,0:T(8,128)} copy(f32[2,8,4,3,32,128]{1,5,3,4,2,0:T(8,128)} %bitcast.32) | data formatting | bytes 6291456 | tf_op jit(solution)/shard_map/transpose | solution.py:557
  208.3 5.0 %convert_element_type.63 = f32[32,3,128,8]{3,2,1,0:T(8,128)} reshape(f32[96,1024]{1,0:T(8,128)S(1)} %convert_element_type.62) | data formatting | bytes 786432 | tf_op jit(solution)/shard_map/convert_element_type | solution.py:558
  213.3 4.4 %copy.40 = f32[8,3,32,128]{3,2,1,0:T(8,128)S(1)} copy(f32[8,3,32,128]{0,3,1,2:T(8,128)} %bitcast.34) | data formatting | bytes 786432 | tf_op jit(solution)/shard_map/transpose | solution.py:559
  217.7 3.3 %convert_multiply_fusion.1.data = f32[8,2,384,128]{3,2,1,0:T(8,128)} fusion(f16[8,2,384,128]{3,2,1,0:T(8,128)(2,1)} %all-to-all-done, f32[]{:T(128)S(6)} %div.14), kind=kLoop, calls=%fused_computation.4 | loop fusion | flops 1572864 | bytes 4718596 | tf_op jit(solution)/shard_map/mul | solution.py:529
  221.1 1.3 broadcast_in_dim.14
  222.4 12.2 %rows_both_ways.1 = f32[8,2,384,128]{3,2,1,0:T(8,128)} custom-call(f32[8,2,384,128]{3,2,1,0:T(8,128)} %convert_multiply_fusion.1.data, f32[8,384,128]{2,1,0:T(8,128)} %bitcast.37, f32[2,8,384,128]{3,2,1,0:T(8,128)} %bitcast.35, bf16[2,256,256]{2,1,0:T(8,128)(2,1)} %constant.75.clone.forward, bf16[2,256,256]{2,1,0:T(8,128)(2,1)} %constant.76.clone.inverse, ...), custom_call_target="tpu_custom_call" | custom-call | tf_op jit(solution)/shard_map/rows_both_ways/pallas_call | solution.py:440
  234.5 3.4 %multiply_convert_fusion = f16[8,2,384,128]{3,2,1,0:T(8,128)(2,1)} fusion(f32[8,2,384,128]{3,2,1,0:T(8,128)} %rows_both_ways.1, f32[]{:T(128)S(6)} %div.15), kind=kLoop, calls=%fused_computation.3 | loop fusion | flops 1572864 | bytes 4718596 | tf_op jit(solution)/shard_map/convert_element_type | solution.py:527
  238.0 6.0 %all-to-all-start.1 = ((f16[8,2,384,128]{3,2,1,0:T(8,128)(2,1)}), f16[8,2,384,128]{3,2,1,0:T(8,128)(2,1)S(1)}, u32[]{:S(2)}, u32[]{:S(2)}) async-start(f16[8,2,384,128]{3,2,1,0:T(8,128)(2,1)} %multiply_convert_fusion), calls=%async_computation.1 | async-start | bytes 3145728 | tf_op jit(solution)/shard_map/all_to_all | solution.py:528
  244.0 37.1 %all-to-all-done.1 = f16[8,2,384,128]{3,2,1,0:T(8,128)(2,1)S(1)} async-done(((f16[8,2,384,128]{3,2,1,0:T(8,128)(2,1)}), f16[8,2,384,128]{3,2,1,0:T(8,128)(2,1)S(1)}, u32[]{:S(2)}, u32[]{:S(2)}) %all-to-all-start.1) | async-done | bytes 1572896 | tf_op jit(solution)/shard_map/all_to_all | solution.py:528
  281.1 1.9 convert_multiply_fusion
  283.0 7.5 %columns_inverse.1 = f32[2,128,768]{2,1,0:T(8,128)} custom-call(f32[8,2,4,3,32,128]{5,4,3,2,1,0:T(8,128)} %bitcast.36, f32[4,2,128,768]{3,2,1,0:T(8,128)} %maps.3, bf16[2,512,512]{2,1,0:T(8,128)(2,1)} %constant.73.clone.matrix, f32[2,3,256]{2,1,0:T(4,128)} %constant.74.clone.table), custom_call_target="tpu_custom_call" | custom-call | tf_op jit(solution)/shard_map/columns_inverse/pallas_call | solution.py:500
  290.5 1.2 slice_select_fusion
  291.6 0.1 collective-permute-start.6
  291.7 1.7 collective-permute-done.6
  293.4 2.0 multiply_add_fusion
  (25 shorter events, 0.1 us)
Async XLA Ops:
  1.2 76.3 %collective-permute-start.3 = (f32[2,128,8]{1,2,0:T(8,128)S(1)}, f32[2,128,8]{1,2,0:T(8,128)S(1)}, u32[]{:S(2)}, u32[]{:S(2)}) collective-permute-start(f32[2,128,8]{1,2,0:T(8,128)S(1)} %broadcast_select_fusion.2), channel_id=1, source_target_pairs={{0,1},{1,0},{2,3},{3,2},{4,5},{5,4},{6,7},{7,6},{8,9},{9,8},{10,11... | collective-permute-start | bytes 24584 | tf_op jit(solution)/shard_map/ppermute | solution.py:203
  1.8 75.7 %collective-permute-start.2 = (f32[2,8,8]{1,2,0:T(8,128)S(1)}, f32[2,8,8]{1,2,0:T(8,128)S(1)}, u32[]{:S(2)}, u32[]{:S(2)}) collective-permute-start(f32[2,8,8]{1,2,0:T(8,128)S(1)} %get-tuple-element.15), channel_id=1, source_target_pairs={{0,3},{1,2},{2,5},{3,4},{4,7},{5,6},{6,9},{7,8},{8,11},{9,10},{10,... | collective-permute-start | bytes 1544 | tf_op jit(solution)/shard_map/ppermute | solution.py:203
  6.3 71.2 %collective-permute-start.4 = (f32[2,8,8]{1,2,0:T(8,128)S(1)}, f32[2,8,8]{1,2,0:T(8,128)S(1)}, u32[]{:S(2)}, u32[]{:S(2)}) collective-permute-start(f32[2,8,8]{1,2,0:T(8,128)S(1)} %get-tuple-element.16), channel_id=1, source_target_pairs={{2,1},{3,0},{4,3},{5,2},{6,5},{7,4},{8,7},{9,6},{10,9},{11,8},{12,... | collective-permute-start | bytes 1544 | tf_op jit(solution)/shard_map/ppermute | solution.py:203
  8.4 70.0 %collective-permute-start = (f32[2,8,384]{2,1,0:T(8,128)S(1)}, f32[2,8,384]{2,1,0:T(8,128)S(1)}, u32[]{:S(2)}, u32[]{:S(2)}) collective-permute-start(f32[2,8,384]{2,1,0:T(8,128)S(1)} %get-tuple-element.12), channel_id=1, source_target_pairs={{0,2},{2,4},{4,6},{6,8},{8,10},{10,12},{12,14},{1,3},{3,5},{5,7},{... | collective-permute-start | bytes 73736 | tf_op jit(solution)/shard_map/ppermute | solution.py:203
  12.6 65.8 %collective-permute-start.1 = (f32[2,8,384]{2,1,0:T(8,128)S(1)}, f32[2,8,384]{2,1,0:T(8,128)S(1)}, u32[]{:S(2)}, u32[]{:S(2)}) collective-permute-start(f32[2,8,384]{2,1,0:T(8,128)S(1)} %get-tuple-element.11), channel_id=1, source_target_pairs={{2,0},{4,2},{6,4},{8,6},{10,8},{12,10},{14,12},{3,1},{5,3},{7,5},{... | collective-permute-start | bytes 73736 | tf_op jit(solution)/shard_map/ppermute | solution.py:203
  74.3 44.8 %copy-start.8 = (bf16[9,64,2]{1,2,0:T(2,128)(2,1)S(1)}, bf16[9,64,2]{1,2,0:T(2,128)(2,1)}, u32[]{:S(2)}) copy-start(bf16[9,64,2]{1,2,0:T(2,128)(2,1)} %param.23) | copy-start | bytes 6916
  74.4 45.5 %copy-start.1 = (bf16[1,9,64,64]{3,2,1,0:T(8,128)(2,1)S(1)}, bf16[1,9,64,64]{3,2,1,0:T(8,128)(2,1)}, u32[]{:S(2)}) copy-start(bf16[1,9,64,64]{3,2,1,0:T(8,128)(2,1)} %param.24) | copy-start | bytes 221188
  74.4 46.3 %copy-start.9 = (bf16[9,2,64]{2,1,0:T(2,128)(2,1)S(1)}, bf16[9,2,64]{2,1,0:T(2,128)(2,1)}, u32[]{:S(2)}) copy-start(bf16[9,2,64]{2,1,0:T(2,128)(2,1)} %param.25) | copy-start | bytes 6916
  78.4 0.6 copy-start.6
  79.0 0.6 copy-start.7
  118.9 4.5 %collective-permute-start.5 = (f32[2,128,384]{2,1,0:T(8,128)}, f32[2,128,384]{2,1,0:T(8,128)S(1)}, u32[]{:S(2)}, u32[]{:S(2)}) collective-permute-start(f32[2,128,384]{2,1,0:T(8,128)} %get-tuple-element.7.mine), channel_id=1, source_target_pairs={{0,1},{1,0},{2,3},{3,2},{4,5},{5,4},{6,7},{7,6},{8,9},{9,8},{10,11... | collective-permute-start | bytes 1179656 | tf_op jit(solution)/shard_map/ppermute | solution.py:545
  123.4 0.7 copy-start.2
  136.4 81.4 %all-to-all-start = ((f16[8,2,384,128]{3,2,1,0:T(8,128)(2,1)}), f16[8,2,384,128]{3,2,1,0:T(8,128)(2,1)}, u32[]{:S(2)}, u32[]{:S(2)}) async-start(f16[8,2,384,128]{3,2,1,0:T(8,128)(2,1)} %bitcast.10), calls=%async_computation | async-start | bytes 3145728 | tf_op jit(solution)/shard_map/all_to_all | solution.py:528
  178.6 29.7 %copy-start.3 = (s32[96,1024]{1,0:T(8,128)S(1)}, s32[96,1024]{1,0:T(8,128)}, u32[]{:S(2)}) copy-start(s32[96,1024]{1,0:T(8,128)} %param.22) | copy-start | bytes 1179652
  238.0 43.1 %all-to-all-start.1 = ((f16[8,2,384,128]{3,2,1,0:T(8,128)(2,1)}), f16[8,2,384,128]{3,2,1,0:T(8,128)(2,1)S(1)}, u32[]{:S(2)}, u32[]{:S(2)}) async-start(f16[8,2,384,128]{3,2,1,0:T(8,128)(2,1)} %multiply_convert_fusion), calls=%async_computation.1 | async-start | bytes 3145728 | tf_op jit(solution)/shard_map/all_to_all | solution.py:528
  283.0 10.4 %copy-start = (f32[2,128,384]{2,1,0:T(8,128)S(1)}, f32[2,128,384]{2,1,0:T(8,128)}, u32[]{:S(2)}) copy-start(f32[2,128,384]{2,1,0:T(8,128)} %get-tuple-element.7.mine) | copy-start | bytes 1179652
  283.0 10.4 %copy-start.4 = (f32[2,128,384]{2,1,0:T(8,128)S(1)}, f32[2,128,384]{2,1,0:T(8,128)}, u32[]{:S(2)}) copy-start(f32[2,128,384]{2,1,0:T(8,128)} %param.19) | copy-start | bytes 1179652
  283.0 10.4 %copy-start.5 = (f32[2,128,384]{2,1,0:T(8,128)S(1)}, f32[2,128,384]{2,1,0:T(8,128)}, u32[]{:S(2)}) copy-start(f32[2,128,384]{2,1,0:T(8,128)} %get-tuple-element.8) | copy-start | bytes 1179652
  291.6 1.8 collective-permute-start.6

commit v2 on v1

--- a/solution.py
+++ b/solution.py
@@ -1,4 +1,5 @@
 import math
+from functools import partial
 
 import jax
 import jax.numpy as jnp
@@ -24,6 +25,7 @@
 BF16 = jnp.bfloat16
 LANES = 128
 EDGE = 8
+INNER = 256
 
 
 def ceil_to(value, step):
@@ -39,34 +41,83 @@
     return choice
 
 
-def pick_taps(choice, kernel):
-    flat = lax.dot_general(
-        jnp.asarray(choice.reshape(-1, 9), BF16),
-        kernel.reshape(9, -1),
-        (((1,), (0,)), ((), ())),
-        preferred_element_type=F32,
-    ).astype(BF16)
-    return flat.reshape(choice.shape[:-1] + kernel.shape[1:])
-
-
-def network_weights(first_kernel, inner_kernel, last_kernel):
-    s, d, x, c, r = np.meshgrid(*map(np.arange, (4, 4, 16, 2, 2)), indexing="ij")
-    first = pick_taps(tap_choice(x - 5 - 2 * s - r, d - c), first_kernel * jnp.asarray(0.5, BF16))
-    first = jnp.transpose(first, (0, 1, 6, 2, 3, 4, 5)).reshape(4, 128, -1)
-    places = []
+def tap_choices():
+    pair = np.eye(2, dtype=np.float32)
+    first, last = [], []
+    for c, r in np.ndindex(2, 2):
+        s, d, x = np.meshgrid(*map(np.arange, (4, 4, 16)), indexing="ij")
+        chosen = tap_choice(x - 5 - 2 * s - r, d - c)
+        first.append(np.einsum("sdxt,hk->shdxtk", chosen, pair).reshape(512, 18))
+        dr, dc = np.meshgrid(np.arange(4), np.arange(4), indexing="ij")
+        chosen = tap_choice(r - dr + 2, c - dc + 2)
+        last.append(np.einsum("yxt,hk->yxhtk", chosen, pair).reshape(32, 18))
+    middle = []
     for cols, rows in (((0, 1), (0, 1)), ((-1, 2), (0, 1)), ((0, 1), (2, -1)), ((-1, 2), (2, -1))):
-        places += [(gamma, rho) for gamma in cols for rho in rows]
-    gamma = np.array([p[0] for p in places])[:, None, None]
-    rho = np.array([p[1] for p in places])[:, None, None]
-    c, r = np.arange(2)[None, :, None], np.arange(2)[None, None, :]
-    rows, cols = np.broadcast_arrays(rho - r + 1, gamma - c + 1)
-    inner = pick_taps(tap_choice(rows, cols), inner_kernel * jnp.asarray(0.5, BF16))
+        for gamma in cols:
+            for rho in rows:
+                taps = []
+                for c, r in np.ndindex(2, 2):
+                    a, b = rho - r + 1, gamma - c + 1
+                    taps.append(3 * a + b if 0 <= a < 3 and 0 <= b < 3 else None)
+                middle.append(taps)
+    return np.stack(first), middle, np.stack(last)
+
+
+def weights_kernel(cols, height, k1, k2, k3, choice1, choice3, first, inner, last, bounds):
+    _, middle, _ = tap_choices()
+    ch = k1.shape[1]
+    parts = [mm(choice1[i], k1[...]) for i in range(4)]
+    first[...] = (0.5 * jnp.concatenate(parts, axis=1)).astype(BF16).reshape(first.shape)
+    turned = [(0.5 * jnp.transpose(k2[t].astype(F32))).astype(BF16) for t in range(9)]
+    zero = jnp.zeros((ch, ch), BF16)
+    for p, taps in enumerate(middle):
+        row = [zero if t is None else turned[t] for t in taps]
+        inner[p * ch : (p + 1) * ch, :] = jnp.concatenate(row, axis=1)
+    parts = [mm(choice3[i], k3[...]) for i in range(4)]
+    last[...] = jnp.concatenate(parts, axis=1).astype(BF16)
+
+    def top(value, axes):
+        for axis in axes:
+            value = jnp.max(value, axis=axis, keepdims=True)
+        return value
+
+    gain1 = top(jnp.sum(jnp.abs(k1[...].astype(F32)), axis=0, keepdims=True), (1,))
+    gain2 = sum(jnp.abs(k2[t].astype(F32)) for t in range(9))
+    gain2 = top(jnp.sum(gain2, axis=1, keepdims=True), (0,))
+    gain3 = jnp.sum(jnp.abs(k3[...].astype(F32)), axis=1, keepdims=True)
+    odd = lax.rem(lax.broadcasted_iota(jnp.int32, gain3.shape, 0), 2) == 1
+    gain3 = jnp.maximum(
+        jnp.sum(jnp.where(odd, gain3, 0.0), axis=0, keepdims=True),
+        jnp.sum(jnp.where(odd, 0.0, gain3), axis=0, keepdims=True),
+    )
+    predicted = 1.1 * NOISY_MAX * gain1 * gain2 * gain3
+    clean = (NOISY_MAX + SIGMA_NOW * predicted) / SCALE_NOW
+    spectra = 1.1 * math.sqrt(cols) * 2.0 * MAPS_MAX * clean
+    lines = 1.1 * math.sqrt(height) * (spectra + math.sqrt(2.0) * MEASURED_MAX)
+    bounds[...] = jnp.concatenate(
+        [jnp.broadcast_to(spectra, (4, LANES)), jnp.broadcast_to(lines, (4, LANES))], axis=0
+    )
+
+
+def network_weights(first_kernel, inner_kernel, last_kernel, cols, height):
     ch = inner_kernel.shape[1]
-    inner = jnp.transpose(inner, (0, 4, 1, 2, 3)).reshape(16 * ch, 4 * ch)
-    dr, dc, c, r = np.meshgrid(*map(np.arange, (4, 4, 2, 2)), indexing="ij")
-    last = pick_taps(tap_choice(r - dr + 2, c - dc + 2), last_kernel)
-    last = jnp.transpose(last, (0, 1, 4, 2, 3, 5)).reshape(32, -1)
-    return first, inner, last
+    choice1, _, choice3 = tap_choices()
+    k1 = jnp.transpose(first_kernel, (0, 2, 1)).reshape(18, ch)
+    shapes = ((4, 128, 4 * ch), (16 * ch, 4 * ch), (32, 4 * ch))
+    first, inner, last, bounds = pl.pallas_call(
+        partial(weights_kernel, cols, height),
+        out_shape=[jax.ShapeDtypeStruct(d, BF16) for d in shapes]
+        + [jax.ShapeDtypeStruct((8, LANES), F32)],
+        cost_estimate=pl.CostEstimate(flops=10**7, bytes_accessed=10**6, transcendentals=0),
+        name="weights",
+    )(
+        k1,
+        inner_kernel,
+        last_kernel.reshape(18, ch),
+        jnp.asarray(choice1, BF16),
+        jnp.asarray(choice3, BF16),
+    )
+    return (first, inner, last), bounds[0, 0], bounds[4, 0]
 
 
 def split3(value):
@@ -110,7 +161,7 @@
         sel = jnp.where(w == 2 * k - 3 + d, 1.0, 0.0).astype(BF16)
         sel_side = jnp.where(e == 2 * ke - 3 + d, 1.0, 0.0).astype(BF16)
         for ch in range(2):
-            q[2 * d + ch] = mm(tile[ch].astype(BF16), sel) + mm(side[ch].astype(BF16), sel_side)
+            q[4 * ch + d] = mm(tile[ch].astype(BF16), sel) + mm(side[ch].astype(BF16), sel_side)
 
     ks = lax.broadcasted_iota(jnp.int32, (used, 256), 0)
     drop_low = jnp.where(flags[2] != 0, 0, -1)
@@ -428,13 +479,15 @@
         out[a, 1] = im
 
 
-def rows_both_ways(data, kept, target):
+def rows_both_ways(data, kept, target, first_line):
     radix, _, count, _ = data.shape
+    pencil = kept.shape[1]
     c, s = fourier_parts(LANES, 1.0 / math.sqrt(radix * LANES))
     forward = halves(np.block([[c, -s], [s, c]]))
     inverse = halves(np.block([[c, s], [-s, c]]))
     table = turn_table(radix, LANES)
-    block = 48 if count % 48 == 0 else 8
+    block = max(b for b in range(8, 56, 8) if pencil % b == 0)
+    offset, repeat = first_line // block, pencil // block
     vmem = pl.BlockSpec(memory_space=pltpu.VMEM)
     spec = pl.BlockSpec((radix, 2, block, LANES), lambda i: (0, 0, i, 0))
     return pl.pallas_call(
@@ -443,8 +496,8 @@
         grid=(count // block,),
         in_specs=[
             spec,
-            pl.BlockSpec((radix, block, LANES), lambda i: (0, i, 0)),
-            pl.BlockSpec((2, radix, block, LANES), lambda i: (0, 0, i, 0)),
+            pl.BlockSpec((radix, block, LANES), lambda i: (0, lax.rem(i + offset, repeat), 0)),
+            pl.BlockSpec((2, radix, block, LANES), lambda i: (0, 0, i + offset, 0)),
             vmem,
             vmem,
             vmem,
@@ -512,15 +565,74 @@
     )(data, maps, jnp.asarray(matrix), jnp.asarray(table))
 
 
-def send_bounds(first_kernel, inner_kernel, last_kernel, cols, height):
-    def gain(kernel):
-        return jnp.max(jnp.sum(jnp.abs(kernel.astype(F32)), axis=(0, 2))) * 1.02
-
-    predicted = NOISY_MAX * gain(first_kernel) * gain(inner_kernel) * gain(last_kernel)
-    clean = (NOISY_MAX + SIGMA_NOW * predicted) / SCALE_NOW
-    spectra = 1.1 * math.sqrt(cols) * 2.0 * MAPS_MAX * clean
-    lines = 1.1 * math.sqrt(height) * (spectra + math.sqrt(2.0) * MEASURED_MAX)
-    return spectra, lines
+def target_kernel(radix3, *refs):
+    tiles = (len(refs) - 4) // 2
+    measured, sampled = refs[:tiles], refs[tiles : 2 * tiles]
+    target, kept, lines, order = refs[2 * tiles :]
+    radix, pencil, _ = kept.shape
+    count, height = lines.shape
+    coils = count // pencil
+    per = pencil // radix3
+
+    @pl.when(pl.program_id(0) == 0)
+    def _():
+        source = lax.broadcasted_iota(jnp.int32, (height, LANES), 0)
+        place = lax.broadcasted_iota(jnp.int32, (height, LANES), 1)
+        for q in range(radix):
+            order[:, q * LANES : (q + 1) * LANES] = jnp.where(
+                source == radix * place + q, 1.0, 0.0
+            ).astype(BF16)
+        for t in range(tiles):
+            for q in range(radix3):
+                lines[q * per : (q + 1) * per, t * LANES : (t + 1) * LANES] = sampled[t][
+                    pl.ds(q, per, stride=radix3), :
+                ].astype(F32)
+        picked = mm(lines[0:pencil, :].astype(BF16), order[...])
+        for q in range(radix):
+            kept[q] = picked[:, q * LANES : (q + 1) * LANES]
+
+    for t in range(tiles):
+        for c in range(coils):
+            for q in range(radix3):
+                start = c * pencil + q * per
+                lines[start : start + per, t * LANES : (t + 1) * LANES] = measured[t][
+                    0, pl.ds(q * coils + c, per, stride=radix3 * coils), :
+                ]
+    high, low = split2(lines[...])
+    for q in range(0, radix, 2):
+        width = min(2, radix - q) * LANES
+        part = order[:, q * LANES : q * LANES + width]
+        picked = mm(high, part) + mm(low, part)
+        for k in range(0, width, LANES):
+            target[0, q + k // LANES] = picked[:, k : k + LANES]
+
+
+def prepare_target(measured, sampled, radix3):
+    _, pencil, coils, height = measured.shape
+    radix = height // LANES
+    count = pencil * coils
+    measured = measured.reshape(2, count, height)
+    return pl.pallas_call(
+        partial(target_kernel, radix3),
+        out_shape=(
+            jax.ShapeDtypeStruct((2, radix, count, LANES), F32),
+            jax.ShapeDtypeStruct((radix, pencil, LANES), F32),
+        ),
+        grid=(2,),
+        in_specs=[
+            pl.BlockSpec((1, count, LANES), lambda i, t=t: (i, 0, t)) for t in range(radix)
+        ]
+        + [pl.BlockSpec((pencil, LANES), lambda i, t=t: (0, t)) for t in range(radix)],
+        out_specs=(
+            pl.BlockSpec((1, radix, count, LANES), lambda i: (i, 0, 0, 0)),
+            pl.BlockSpec((radix, pencil, LANES), lambda i: (0, 0, 0)),
+        ),
+        scratch_shapes=[pltpu.VMEM((count, height), F32), pltpu.VMEM((height, height), BF16)],
+        cost_estimate=pl.CostEstimate(
+            flops=8 * count * height * height, bytes_accessed=16 * count * height, transcendentals=0
+        ),
+        name="target",
+    )(*[measured] * radix, *[sampled] * radix)
 
 
 def exchange(value, bound):
@@ -535,31 +647,25 @@
     groups = lax.axis_size("gz")
     coils, _, rows, cols = coil_maps.shape
     height = measured.shape[3]
-    radix, inner = cols // 256, 256
+    radix, inner = cols // INNER, INNER
     per = inner // groups
     row_radix = height // LANES
 
-    weights = network_weights(first_kernel, inner_kernels[0], last_kernel)
+    weights, spectra_bound, lines_bound = network_weights(
+        first_kernel, inner_kernels[0], last_kernel, cols, height
+    )
     top, bottom, side = halo(noisy_image)
     predicted, clean = run_network(noisy_image, top, bottom, side, edge_flags(), weights)
     other = lax.ppermute(clean, "col", [(0, 1), (1, 0)])
 
-    spectra_bound, lines_bound = send_bounds(
-        first_kernel, inner_kernels[0], last_kernel, cols, height
-    )
     spectra = columns_forward(clean, other, coil_maps, groups)
     spectra = spectra.reshape(groups, 2, coils * radix * per, rows)
     arrived = exchange(spectra, spectra_bound)
     if rows != LANES:
         arrived = jnp.transpose(arrived, (1, 2, 0, 3)).reshape(2, -1, row_radix, LANES)
         arrived = jnp.transpose(arrived, (2, 0, 1, 3))
-    target = measured.reshape(2, per, radix, coils, LANES, row_radix)
-    target = jnp.transpose(target, (0, 5, 3, 2, 1, 4)).reshape(2, row_radix, -1, LANES)
-    kept = sampled.reshape(per, radix, LANES, row_radix).astype(F32)
-    kept = jnp.transpose(kept, (3, 1, 0, 2))[:, None]
-    kept = jnp.broadcast_to(kept, (row_radix, coils, radix, per, LANES))
-    kept = kept.reshape(row_radix, -1, LANES)
-    lines = rows_both_ways(arrived, kept, target)
+    target, kept = prepare_target(measured, sampled, radix)
+    lines = rows_both_ways(arrived, kept, target, 0)
     if rows != LANES:
         lines = jnp.transpose(lines, (1, 2, 0, 3)).reshape(2, -1, groups, rows)
         lines = jnp.transpose(lines, (2, 0, 1, 3))

time: 297 us -> 194 us (0.65)
  local copies, waits for them, and re-layouts: 138 us -> 12.9 us
  waiting for transfers between devices: 38.8 us -> 61.7 us
  Pallas kernels: 67.8 us -> 77.7 us
  other arithmetic: 19.8 us -> 14.6 us
  matrix products: 3 us -> 0 us
    reshape x10 -> x3, local copies, waits for them, and re-layouts: 74.1 us -> 7.51 us  [the longest x1 4.92 us: prepare_target(): measured = measured.reshape(2, count, height)]
    transpose x3 -> x0, local copies, waits for them, and re-layouts: 48.8 us -> none  [the longest x1 29.7 us: local(): jnp.transpose(target, (0, 5, 3, 2, 1, 4)).reshape(2, row_radix, -1, LANES)]
    all_to_all x2, waiting for transfers between devices: 37.1 us -> 60 us  [exchange(): half = lax.all_to_all(half, 'gz', split_axis=0, concat_axis=0, tiled=True)]
    pallas_call x0 -> x2, Pallas kernels: none -> 10 us  [the longest x1 7.6 us: prepare_target(): pl.pallas_call(partial(target_kernel, radix3), out_shape=(jax.ShapeDtypeS...]
    convert_element_type x2 -> x0, local copies, waits for them, and re-layouts: 5.15 us -> none  [the longest x1 4.98 us: local(): kept = sampled.reshape(per, radix, LANES, row_radix).astype(F32)]
    unnamed x23 -> x14, local copies, waits for them, and re-layouts: 5.82 us -> 1.48 us
    all_to_all x2, starting transfers between devices: 13.6 us -> 9.99 us  [exchange(): half = lax.all_to_all(half, 'gz', split_axis=0, concat_axis=0, tiled=True)]
    dot_general x3 -> x0, matrix products: 3 us -> none  [pick_taps(): lax.dot_general(jnp.asarray(choice.reshape(-1, 9), BF16), kernel.reshape(...]
  transfers between devices with their start and end apart: 9 -> 9, of which waited for: 2 -> 3; matrix products, arithmetic and copies ran while one was open for 48% -> 6% of each run, Pallas kernels for 0% -> 5%
where the time goes in v2:
time: 194 us; the launch traced here: 192 us
  Pallas kernels  77.7 us (40%)
  waiting for transfers between devices  61.7 us (32%)
  starting transfers between devices  22.9 us (12%)
  other arithmetic  14.6 us (8%)
  local copies, waits for them, and re-layouts  12.9 us (7%)
  between operations  2.64 us (1%)
    all_to_all x2, waiting for transfers between devices, exchange(): half = lax.all_to_all(half, 'gz', split_axis=0, concat_axis=0, tiled=True)  60 us
    pallas_call x1, Pallas kernels, run_network(): pl.pallas_call(network_kernel, out_shape=(shape, shape), in_specs=[pl.Blo...  39.3 us
    ppermute x5, starting transfers between devices, move(): return lax.ppermute(value, axis, pairs)  12.8 us
    pallas_call x1, Pallas kernels, rows_both_ways(): pl.pallas_call(rows_kernel, out_shape=jax.ShapeDtypeStruct(data.shape, F3...  12.1 us
    all_to_all x2, starting transfers between devices, exchange(): half = lax.all_to_all(half, 'gz', split_axis=0, concat_axis=0, tiled=True)  9.99 us
    pallas_call x1, Pallas kernels, columns_forward(): pl.pallas_call(columns_forward_kernel, out_shape=jax.ShapeDtypeStruct((gr...  8.77 us
    pallas_call x1, Pallas kernels, prepare_target(): pl.pallas_call(partial(target_kernel, radix3), out_shape=(jax.ShapeDtypeS...  7.6 us
    pallas_call x1, Pallas kernels, columns_inverse(): pl.pallas_call(columns_inverse_kernel, out_shape=jax.ShapeDtypeStruct((2,...  7.49 us
  transfers between devices with their start and end apart: 9, of which 3 were waited for; matrix products, arithmetic and copies ran while one was open for 6% of the time, Pallas kernels for 5%

profile of v2, /device:TPU:0, one launch (start us, length us, event | category | flops | bytes accessed | tf_op | source)
XLA Modules:
  0.0 192.5 jit_solution(13290495431910638725)
XLA Ops:
  0.0 0.8 fusion.1
  0.8 4.9 %collective-permute-start = (f32[2,8,384]{2,1,0:T(8,128)S(1)}, f32[2,8,384]{2,1,0:T(8,128)S(1)}, u32[]{:S(2)}, u32[]{:S(2)}) collective-permute-start(f32[2,8,384]{2,1,0:T(8,128)S(1)} %get-tuple-element.24), channel_id=1, source_target_pairs={{0,2},{2,4},{4,6},{6,8},{8,10},{10,12},{12,14},{1,3},{3,5},{5,7},{... | collective-permute-start | bytes 73736 | tf_op jit(solution)/shard_map/ppermute | solution.py:254
  5.7 1.3 collective-permute-start.1
  7.0 1.1 fusion
  8.0 0.1 copy.21
  8.1 0.1 copy.22
  8.2 0.1 collective-permute-start.3
  8.2 0.1 fusion.2
  8.3 1.3 collective-permute-start.4
  9.6 5.3 %collective-permute-start.2 = (f32[2,8,8]{1,2,0:T(8,128)S(1)}, f32[2,8,8]{1,2,0:T(8,128)S(1)}, u32[]{:S(2)}, u32[]{:S(2)}) collective-permute-start(f32[2,8,8]{1,2,0:T(8,128)S(1)} %get-tuple-element.27), channel_id=1, source_target_pairs={{0,3},{1,2},{2,5},{3,4},{4,7},{5,6},{6,9},{7,8},{8,11},{9,10},{10,... | collective-permute-start | bytes 1544 | tf_op jit(solution)/shard_map/ppermute | solution.py:254
  14.9 0.6 add_convert_fusion.flags
  15.5 1.3 reshape.24.k1
  16.8 1.3 reshape.25.k3
  18.1 2.4 %weights.1 = (bf16[4,128,256]{2,1,0:T(8,128)(2,1)}, bf16[1024,256]{1,0:T(8,128)(2,1)}, bf16[32,256]{1,0:T(8,128)(2,1)}, f32[8,128]{1,0:T(8,128)}) custom-call(bf16[18,64]{1,0:T(8,128)(2,1)} %reshape.24.k1, bf16[9,64,64]{2,1,0:T(8,128)(2,1)} %bitcast.13, bf16[18,64]{1,0:T(8,128)(2,1)} %reshape.25.k3, bf16[4,512,18]{2,1,0:T(8,128)(2,1)} %constant.45.clone.choice1, ...), custom_call_target="tpu_custom_call" | custom-call | flops 10000000 | bytes 1000000 | tf_op jit(solution)/shard_map/weights/pallas_call | solution.py:107
  20.5 0.0 collective-permute-done.4
  20.5 0.0 collective-permute-done.2
  20.5 0.0 collective-permute-done.3
  20.5 0.1 broadcast_select_fusion.1
  20.6 0.8 copy.20.side
  21.4 0.0 collective-permute-done.top
  21.4 0.0 copy-start.4
  21.4 0.0 collective-permute-done.1.bottom
  21.4 0.0 copy-start.5
  21.4 0.6 copy-done.4
  22.0 0.0 copy-done.5
  22.0 39.3 %network.1 = (f32[2,128,384]{2,1,0:T(8,128)}, f32[2,128,384]{2,1,0:T(8,128)}) custom-call(s32[4]{0:T(128)} %add_convert_fusion.flags, f32[2,8,384]{2,1,0:T(8,128)} %copy-done.4, f32[2,128,384]{2,1,0:T(8,128)} %center.1, f32[2,8,384]{2,1,0:T(8,128)} %copy-done.5, f32[2,144,16]{2,1,0:T(8,128)} %copy.20.side, bf16[4,128,256]{2,1,0:T(8,128)(2,1)} %get-tuple-element.13.first, ...), custom_call_target="tpu_custom_call" | custom-call | tf_op jit(solution)/shard_map/network/pallas_call | solution.py:236
  61.3 0.0 collective-permute-start.5
  61.3 1.3 fusion.3
  63.3 0.0 collective-permute-done.5.other
  63.3 0.0 copy-start.1
  63.3 0.7 copy-done.1
  64.0 8.8 %columns_forward.1 = f32[8,2,4,3,32,128]{5,4,3,2,1,0:T(8,128)} custom-call(s32[1]{0:T(128)S(6)} %broadcast_in_dim.7.first, f32[2,128,384]{2,1,0:T(8,128)} %get-tuple-element.16.mine, f32[2,128,384]{2,1,0:T(8,128)} %copy-done.1, f32[4,2,128,768]{3,2,1,0:T(8,128)} %maps.3, bf16[2,512,512]{2,1,0:T(8,128)(2,1)} %constant.47.clone.matrix, ...), custom_call_target="tpu_custom_call" | custom-call | tf_op jit(solution)/shard_map/columns_forward/pallas_call | solution.py:436
  72.8 3.4 %multiply_convert_fusion.1 = f16[8,2,4,3,32,128]{5,4,3,2,1,0:T(8,128)(2,1)} fusion(f32[8,2,4,3,32,128]{5,4,3,2,1,0:T(8,128)} %columns_forward.1, f32[]{:T(128)} %bitcast.6), kind=kLoop, calls=%fused_computation.3 | loop fusion | flops 1572864 | bytes 4718596 | tf_op jit(solution)/shard_map/convert_element_type | solution.py:639
  76.2 6.4 %all-to-all-start = ((f16[8,2,384,128]{3,2,1,0:T(8,128)(2,1)}), f16[8,2,384,128]{3,2,1,0:T(8,128)(2,1)S(1)}, u32[]{:S(2)}, u32[]{:S(2)}) async-start(f16[8,2,384,128]{3,2,1,0:T(8,128)(2,1)} %bitcast.7), calls=%async_computation | async-start | bytes 3145728 | tf_op jit(solution)/shard_map/all_to_all | solution.py:640
  83.2 4.9 %reshape.26.refs_0_.refs_1_.refs_2_.refs_3_.refs_4_.refs_5_.refs_6_.refs_7_ = f32[2,384,1024]{2,1,0:T(8,128)} reshape(f32[2,96,4,1024]{3,2,1,0:T(4,128)} %param.20) | data formatting | bytes 6291456 | tf_op jit(solution)/shard_map/reshape | solution.py:614
  88.8 7.6 %target.1 = (f32[2,8,384,128]{3,2,1,0:T(8,128)}, f32[8,96,128]{2,1,0:T(8,128)}) custom-call(f32[2,384,1024]{2,1,0:T(8,128)} %reshape.26.refs_0_.refs_1_.refs_2_.refs_3_.refs_4_.refs_5_.refs_6_.refs_7_, f32[2,384,1024]{2,1,0:T(8,128)} %reshape.26.refs_0_.refs_1_.refs_2_.refs_3_.refs_4_.refs_5_.refs_6_.refs_7_, ...), custom_call_target="tpu_custom_call" | custom-call | flops 3221225472 | bytes 6291456 | tf_op jit(solution)/shard_map/target/pallas_call | solution.py:615
  96.4 23.4 %all-to-all-done = f16[8,2,384,128]{3,2,1,0:T(8,128)(2,1)S(1)} async-done(((f16[8,2,384,128]{3,2,1,0:T(8,128)(2,1)}), f16[8,2,384,128]{3,2,1,0:T(8,128)(2,1)S(1)}, u32[]{:S(2)}, u32[]{:S(2)}) %all-to-all-start) | async-done | bytes 1572896 | tf_op jit(solution)/shard_map/all_to_all | solution.py:640
  119.8 2.0 %convert_multiply_fusion.1.data = f32[8,2,384,128]{3,2,1,0:T(8,128)} fusion(f16[8,2,384,128]{3,2,1,0:T(8,128)(2,1)S(1)} %all-to-all-done, f32[]{:T(128)} %bitcast.8), kind=kLoop, calls=%fused_computation.2 | loop fusion | flops 1572864 | bytes 4718596 | tf_op jit(solution)/shard_map/mul | solution.py:641
  121.7 12.1 %rows_both_ways.1 = f32[8,2,384,128]{3,2,1,0:T(8,128)} custom-call(f32[8,2,384,128]{3,2,1,0:T(8,128)} %convert_multiply_fusion.1.data, f32[8,96,128]{2,1,0:T(8,128)} %get-tuple-element.18.kept, f32[2,8,384,128]{3,2,1,0:T(8,128)} %get-tuple-element.19.target, bf16[2,256,256]{2,1,0:T(8,128)(2,1)} %constant.49.clone.forward, ...), custom_call_target="tpu_custom_call" | custom-call | tf_op jit(solution)/shard_map/rows_both_ways/pallas_call | solution.py:493
  133.9 3.5 %multiply_convert_fusion = f16[8,2,384,128]{3,2,1,0:T(8,128)(2,1)} fusion(f32[8,2,384,128]{3,2,1,0:T(8,128)} %rows_both_ways.1, f32[]{:T(128)} %bitcast.9), kind=kLoop, calls=%fused_computation.1 | loop fusion | flops 1572864 | bytes 4718596 | tf_op jit(solution)/shard_map/convert_element_type | solution.py:639
  137.3 3.6 %all-to-all-start.1 = ((f16[8,2,384,128]{3,2,1,0:T(8,128)(2,1)}), f16[8,2,384,128]{3,2,1,0:T(8,128)(2,1)S(1)}, u32[]{:S(2)}, u32[]{:S(2)}) async-start(f16[8,2,384,128]{3,2,1,0:T(8,128)(2,1)} %multiply_convert_fusion), calls=%async_computation.1 | async-start | bytes 3145728 | tf_op jit(solution)/shard_map/all_to_all | solution.py:640
  141.5 36.6 %all-to-all-done.1 = f16[8,2,384,128]{3,2,1,0:T(8,128)(2,1)S(1)} async-done(((f16[8,2,384,128]{3,2,1,0:T(8,128)(2,1)}), f16[8,2,384,128]{3,2,1,0:T(8,128)(2,1)S(1)}, u32[]{:S(2)}, u32[]{:S(2)}) %all-to-all-start.1) | async-done | bytes 1572896 | tf_op jit(solution)/shard_map/all_to_all | solution.py:640
  178.1 1.9 convert_multiply_fusion
  180.0 0.0 copy-start
  180.0 0.0 copy-start.2
  180.0 0.0 copy-start.3
  180.0 7.5 %columns_inverse.1 = f32[2,128,768]{2,1,0:T(8,128)} custom-call(f32[8,2,4,3,32,128]{5,4,3,2,1,0:T(8,128)} %bitcast.12, f32[4,2,128,768]{3,2,1,0:T(8,128)} %maps.3, bf16[2,512,512]{2,1,0:T(8,128)(2,1)} %constant.47.clone.matrix, f32[2,3,256]{2,1,0:T(4,128)} %constant.48.clone.table), custom_call_target="tpu_custom_call" | custom-call | tf_op jit(solution)/shard_map/columns_inverse/pallas_call | solution.py:553
  187.5 1.2 slice_select_fusion
  188.7 0.1 collective-permute-start.6
  188.8 1.7 collective-permute-done.6
  190.5 0.0 copy-done
  190.5 0.0 copy-done.2
  190.5 0.0 copy-done.3
  190.5 2.0 %multiply_add_fusion = f32[2,128,384]{2,1,0:T(8,128)} fusion(f32[2,128,384]{2,1,0:T(8,128)S(1)} %copy-done.2, f32[2,128,384]{2,1,0:T(8,128)S(1)} %copy-done.3, f32[2,128,384]{2,1,0:T(8,128)S(1)} %copy-done, f32[2,128,384]{2,1,0:T(8,128)S(1)} %collective-permute-done.6, f32[2,128,768]{2,1,0:T(8,128)} %columns_inverse.1, pred[]{:T(512)} %eq.17), kind=kLoop, calls=%fused_computation.4 | loop fusion | flops 786432 | bytes 2752513 | tf_op jit(solution)/shard_map/add | solution.py:682
  (2 shorter events, 0.0 us)
Async XLA Ops:
  0.8 20.6 %collective-permute-start = (f32[2,8,384]{2,1,0:T(8,128)S(1)}, f32[2,8,384]{2,1,0:T(8,128)S(1)}, u32[]{:S(2)}, u32[]{:S(2)}) collective-permute-start(f32[2,8,384]{2,1,0:T(8,128)S(1)} %get-tuple-element.24), channel_id=1, source_target_pairs={{0,2},{2,4},{4,6},{6,8},{8,10},{10,12},{12,14},{1,3},{3,5},{5,7},{... | collective-permute-start | bytes 73736 | tf_op jit(solution)/shard_map/ppermute | solution.py:254
  5.7 15.7 %collective-permute-start.1 = (f32[2,8,384]{2,1,0:T(8,128)S(1)}, f32[2,8,384]{2,1,0:T(8,128)S(1)}, u32[]{:S(2)}, u32[]{:S(2)}) collective-permute-start(f32[2,8,384]{2,1,0:T(8,128)S(1)} %get-tuple-element.23), channel_id=1, source_target_pairs={{2,0},{4,2},{6,4},{8,6},{10,8},{12,10},{14,12},{3,1},{5,3},{7,5},{... | collective-permute-start | bytes 73736 | tf_op jit(solution)/shard_map/ppermute | solution.py:254
  8.2 12.3 %collective-permute-start.3 = (f32[2,128,8]{1,2,0:T(8,128)S(1)}, f32[2,128,8]{1,2,0:T(8,128)S(1)}, u32[]{:S(2)}, u32[]{:S(2)}) collective-permute-start(f32[2,128,8]{1,2,0:T(8,128)S(1)} %broadcast_select_fusion.2), channel_id=1, source_target_pairs={{0,1},{1,0},{2,3},{3,2},{4,5},{5,4},{6,7},{7,6},{8,9},{9,8},{10,11... | collective-permute-start | bytes 24584 | tf_op jit(solution)/shard_map/ppermute | solution.py:254
  8.3 12.2 %collective-permute-start.4 = (f32[2,8,8]{1,2,0:T(8,128)S(1)}, f32[2,8,8]{1,2,0:T(8,128)S(1)}, u32[]{:S(2)}, u32[]{:S(2)}) collective-permute-start(f32[2,8,8]{1,2,0:T(8,128)S(1)} %get-tuple-element.28), channel_id=1, source_target_pairs={{2,1},{3,0},{4,3},{5,2},{6,5},{7,4},{8,7},{9,6},{10,9},{11,8},{12,... | collective-permute-start | bytes 1544 | tf_op jit(solution)/shard_map/ppermute | solution.py:254
  9.6 10.9 %collective-permute-start.2 = (f32[2,8,8]{1,2,0:T(8,128)S(1)}, f32[2,8,8]{1,2,0:T(8,128)S(1)}, u32[]{:S(2)}, u32[]{:S(2)}) collective-permute-start(f32[2,8,8]{1,2,0:T(8,128)S(1)} %get-tuple-element.27), channel_id=1, source_target_pairs={{0,3},{1,2},{2,5},{3,4},{4,7},{5,6},{6,9},{7,8},{8,11},{9,10},{10,... | collective-permute-start | bytes 1544 | tf_op jit(solution)/shard_map/ppermute | solution.py:254
  21.4 0.6 copy-start.4
  21.4 0.6 copy-start.5
  61.3 2.0 %collective-permute-start.5 = (f32[2,128,384]{2,1,0:T(8,128)}, f32[2,128,384]{2,1,0:T(8,128)S(1)}, u32[]{:S(2)}, u32[]{:S(2)}) collective-permute-start(f32[2,128,384]{2,1,0:T(8,128)} %get-tuple-element.16.mine), channel_id=1, source_target_pairs={{0,1},{1,0},{2,3},{3,2},{4,5},{5,4},{6,7},{7,6},{8,9},{9,8},{10,11... | collective-permute-start | bytes 1179656 | tf_op jit(solution)/shard_map/ppermute | solution.py:659
  63.3 0.7 copy-start.1
  76.2 43.5 %all-to-all-start = ((f16[8,2,384,128]{3,2,1,0:T(8,128)(2,1)}), f16[8,2,384,128]{3,2,1,0:T(8,128)(2,1)S(1)}, u32[]{:S(2)}, u32[]{:S(2)}) async-start(f16[8,2,384,128]{3,2,1,0:T(8,128)(2,1)} %bitcast.7), calls=%async_computation | async-start | bytes 3145728 | tf_op jit(solution)/shard_map/all_to_all | solution.py:640
  137.3 40.8 %all-to-all-start.1 = ((f16[8,2,384,128]{3,2,1,0:T(8,128)(2,1)}), f16[8,2,384,128]{3,2,1,0:T(8,128)(2,1)S(1)}, u32[]{:S(2)}, u32[]{:S(2)}) async-start(f16[8,2,384,128]{3,2,1,0:T(8,128)(2,1)} %multiply_convert_fusion), calls=%async_computation.1 | async-start | bytes 3145728 | tf_op jit(solution)/shard_map/all_to_all | solution.py:640
  180.0 10.4 %copy-start = (f32[2,128,384]{2,1,0:T(8,128)S(1)}, f32[2,128,384]{2,1,0:T(8,128)}, u32[]{:S(2)}) copy-start(f32[2,128,384]{2,1,0:T(8,128)} %get-tuple-element.16.mine) | copy-start | bytes 1179652
  180.0 10.4 %copy-start.2 = (f32[2,128,384]{2,1,0:T(8,128)S(1)}, f32[2,128,384]{2,1,0:T(8,128)}, u32[]{:S(2)}) copy-start(f32[2,128,384]{2,1,0:T(8,128)} %param.18) | copy-start | bytes 1179652
  180.0 10.4 %copy-start.3 = (f32[2,128,384]{2,1,0:T(8,128)S(1)}, f32[2,128,384]{2,1,0:T(8,128)}, u32[]{:S(2)}) copy-start(f32[2,128,384]{2,1,0:T(8,128)} %get-tuple-element.20) | copy-start | bytes 1179652
  188.7 1.8 collective-permute-start.6

commit v3 on v2

v3 whole, which is shorter than its diff:
```python
import math
from functools import partial

import jax
import jax.numpy as jnp
import ml_dtypes
import numpy as np
from jax import lax
from jax.experimental import pallas as pl
from jax.experimental.pallas import tpu as pltpu
from jax.sharding import PartitionSpec as P

SCALE_NOW = 0.8
SIGMA_NOW = 0.6
STEP_GAIN = 1.0
SCALE_NEXT = 0.9
DIRECT_GAIN = 0.31622776601683794
NOISE_GAIN = 0.3

NOISY_MAX = 6.0
MAPS_MAX = 1.5
MEASURED_MAX = 2.4

F32 = jnp.float32
BF16 = jnp.bfloat16
LANES = 128
EDGE = 8
INNER = 256


def ceil_to(value, step):
    return -(-value // step) * step


def tap_choice(rows, cols):
    choice = np.zeros(rows.shape + (9,), np.float32)
    for index in np.ndindex(rows.shape):
        a, b = rows[index], cols[index]
        if 0 <= a < 3 and 0 <= b < 3:
            choice[index + (3 * a + b,)] = 1.0
    return choice


def tap_choices():
    pair = np.eye(2, dtype=np.float32)
    first, last = [], []
    for c, r in np.ndindex(2, 2):
        s, d, x = np.meshgrid(*map(np.arange, (4, 4, 16)), indexing="ij")
        chosen = tap_choice(x - 5 - 2 * s - r, d - c)
        first.append(np.einsum("sdxt,hk->shdxtk", chosen, pair).reshape(512, 18))
        dr, dc = np.meshgrid(np.arange(4), np.arange(4), indexing="ij")
        chosen = tap_choice(r - dr + 2, c - dc + 2)
        last.append(np.einsum("yxt,hk->yxhtk", chosen, pair).reshape(32, 18))
    middle = []
    for cols, rows in (((0, 1), (0, 1)), ((-1, 2), (0, 1)), ((0, 1), (2, -1)), ((-1, 2), (2, -1))):
        for gamma in cols:
            for rho in rows:
                taps = []
                for c, r in np.ndindex(2, 2):
                    a, b = rho - r + 1, gamma - c + 1
                    taps.append(3 * a + b if 0 <= a < 3 and 0 <= b < 3 else None)
                middle.append(taps)
    return np.stack(first), middle, np.stack(last)


def weights_kernel(cols, height, first_taps, k2, last_taps, choice1, choice3, first, inner, last, scales):
    _, middle, _ = tap_choices()
    ch = k2.shape[1]
    k1 = jnp.concatenate([first_taps[t].astype(F32) for t in range(9)], axis=0).astype(BF16)
    k3 = jnp.concatenate([last_taps[t].astype(F32) for t in range(9)], axis=0).astype(BF16)
    parts = [mm(choice1[i], k1) for i in range(4)]
    first[...] = (0.5 * jnp.concatenate(parts, axis=1)).astype(BF16).reshape(first.shape)
    turned = [(0.5 * jnp.transpose(k2[t].astype(F32))).astype(BF16) for t in range(9)]
    zero = jnp.zeros((ch, ch), BF16)
    for p, taps in enumerate(middle):
        row = [zero if t is None else turned[t] for t in taps]
        inner[p * ch : (p + 1) * ch, :] = jnp.concatenate(row, axis=1)
    parts = [mm(choice3[i], k3) for i in range(4)]
    last[...] = jnp.concatenate(parts, axis=1).astype(BF16)

    def top(value, axes):
        for axis in axes:
            value = jnp.max(value, axis=axis, keepdims=True)
        return value

    gain1 = top(jnp.sum(jnp.abs(k1.astype(F32)), axis=0, keepdims=True), (1,))
    gain2 = sum(jnp.abs(k2[t].astype(F32)) for t in range(9))
    gain2 = top(jnp.sum(gain2, axis=1, keepdims=True), (0,))
    gain3 = jnp.sum(jnp.abs(k3.astype(F32)), axis=1, keepdims=True)
    odd = lax.rem(lax.broadcasted_iota(jnp.int32, gain3.shape, 0), 2) == 1
    gain3 = jnp.maximum(
        jnp.sum(jnp.where(odd, gain3, 0.0), axis=0, keepdims=True),
        jnp.sum(jnp.where(odd, 0.0, gain3), axis=0, keepdims=True),
    )
    predicted = 1.1 * NOISY_MAX * gain1 * gain2 * gain3
    clean = (NOISY_MAX + SIGMA_NOW * predicted) / SCALE_NOW
    spectra = 1.1 * math.sqrt(cols) * 2.0 * MAPS_MAX * clean
    lines = 1.1 * math.sqrt(height) * (spectra + math.sqrt(2.0) * MEASURED_MAX)
    rows = []
    for bound in (spectra, lines):
        rows += [60000.0 / bound, bound / 60000.0]
    scales[...] = jnp.concatenate([jnp.broadcast_to(r, (1, LANES)) for r in rows + rows], axis=0)


def network_weights(first_kernel, inner_kernel, last_kernel, cols, height):
    ch = inner_kernel.shape[1]
    choice1, _, choice3 = tap_choices()
    shapes = ((4, 128, 4 * ch), (16 * ch, 4 * ch), (32, 4 * ch))
    first, inner, last, scales = pl.pallas_call(
        partial(weights_kernel, cols, height),
        out_shape=[jax.ShapeDtypeStruct(d, BF16) for d in shapes]
        + [jax.ShapeDtypeStruct((8, LANES), F32)],
        cost_estimate=pl.CostEstimate(flops=10**7, bytes_accessed=10**6, transcendentals=0),
        name="weights",
    )(
        jnp.transpose(first_kernel, (0, 2, 1)),
        inner_kernel,
        last_kernel,
        jnp.asarray(choice1, BF16),
        jnp.asarray(choice3, BF16),
    )
    return (first, inner, last), scales


def split3(value):
    high = value.astype(BF16)
    rest = value - high.astype(F32)
    middle = rest.astype(BF16)
    return high, middle, (rest - middle.astype(F32)).astype(BF16)


def split2(value):
    high = value.astype(BF16)
    return high, (value - high.astype(F32)).astype(BF16)


def mm(lhs, rhs):
    return lax.dot_general(lhs, rhs, (((1,), (0,)), ((), ())), preferred_element_type=F32)


def mm_nt(lhs, rhs):
    return lax.dot_general(lhs, rhs, (((1,), (1,)), ((), ())), preferred_element_type=F32)


def network_kernel(
    flags, top, center, bottom, side, first, inner, last, pred, clean, tile, q, hid, hid_side, acc
):
    rows, cols = center.shape[1:]
    blocks = rows // 2 + 2
    groups = q.shape[1] // 8 - 1
    used = hid.shape[1]
    step = max(u for u in (1, 2, 3) if blocks % u == 0)

    for ch in range(2):
        tile[ch, 0:8, :] = top[ch, :, 0:cols]
        tile[ch, 8 : 8 + rows, :] = center[ch]
        tile[ch, 8 + rows : 16 + rows, :] = bottom[ch, :, 0:cols]
    edge = jnp.concatenate(
        [
            part
            for ch in range(2)
            for part in (top[ch, :, cols:], side[ch], bottom[ch, :, cols:])
        ],
        axis=0,
    ).astype(BF16)
    w = lax.broadcasted_iota(jnp.int32, (cols, 256), 0)
    k = lax.broadcasted_iota(jnp.int32, (cols, 256), 1)
    e = lax.broadcasted_iota(jnp.int32, (EDGE, 256), 0) + jnp.where(flags[2] != 0, cols, -EDGE)
    ke = lax.broadcasted_iota(jnp.int32, (EDGE, 256), 1)
    for d in range(4):
        sel = jnp.where(w == 2 * k - 3 + d, 1.0, 0.0).astype(BF16)
        sel_side = jnp.where(e == 2 * ke - 3 + d, 1.0, 0.0).astype(BF16)
        both = mm(tile[...].reshape(-1, cols).astype(BF16), sel)
        both += mm(edge, sel_side)
        for ch in range(2):
            q[4 * ch + d] = both[ch * (rows + 16) : (ch + 1) * (rows + 16)]

    end = cols // 2 + 1
    tail = end // 8 * 8
    lines = lax.broadcasted_iota(jnp.int32, (8, 256), 0)
    low = jnp.where((lines == 0) & (flags[2] != 0), 0.0, 1.0)
    high = jnp.where((lines == end - tail) & (flags[3] != 0), 0.0, 1.0)

    def silu_rows(half):
        h = half + half * jnp.tanh(half)
        pieces = []
        for start in range(0, h.shape[0], used):
            pieces += [
                h[start : start + 8] * low,
                h[start + 8 : start + tail],
                h[start + tail : start + tail + 8] * high,
            ]
            if tail + 8 < used:
                pieces.append(h[start + tail + 8 : start + used])
        return jnp.concatenate(pieces, axis=0)

    acc[...] = jnp.zeros(acc.shape, F32)
    hid[0] = jnp.zeros(hid.shape[1:], BF16)
    hid_side[0] = jnp.zeros(hid.shape[1:], BF16)

    def first_layer(t, carry):
        window = q[:, pl.ds(pl.multiple_of(8 * t, 8), 16), :].reshape(128, 256)
        window = jnp.transpose(window)[:used].astype(BF16)
        for s in range(4):
            h = silu_rows(mm(window, first[s]))
            place = 4 * t + s + 1
            hid[place] = h.astype(BF16)
            hid_side[place, :, 0:128] = pltpu.roll(h[:, 128:256], 1, 0).astype(BF16)
            hid_side[place, :, 128:256] = pltpu.roll(h[:, 0:128], used - 1, 0).astype(BF16)
        return carry

    lax.fori_loop(0, groups, first_layer, 0)

    for flag, j in ((0, 0), (1, blocks - 1)):

        @pl.when(flags[flag] != 0)
        def _(j=j):
            hid[j + 1] = jnp.zeros(hid.shape[1:], BF16)
            hid_side[j + 1] = jnp.zeros(hid_side.shape[1:], BF16)

    lane = lax.broadcasted_iota(jnp.int32, (step * used, 256), 1)
    below = lax.rem(lane, 128) < 64

    def next_layers(i, carry):
        j = step * i

        def around(ref, offset):
            return ref[pl.ds(j + offset, step)].reshape(step * used, 256)

        lhs = jnp.concatenate(
            [
                around(hid, 1),
                around(hid_side, 1),
                jnp.where(below, around(hid, 2), around(hid, 0)),
                jnp.where(below, around(hid_side, 2), around(hid_side, 0)),
            ],
            axis=1,
        )
        h = silu_rows(mm(lhs, inner[...])).astype(BF16)
        for u in range(step):
            part = mm_nt(last[...], h[u * used : (u + 1) * used])
            row = j + u
            gone = ((row == 0) & (flags[0] != 0)) | ((row == blocks - 1) & (flags[1] != 0))
            part = part * jnp.where(gone, 0.0, 1.0)
            where = pl.ds(pl.multiple_of(16 * row, 16), 32)
            for c in range(0, used, 128):
                width = min(128, used - c)
                acc[c // 128, where, 0:width] = acc[c // 128, where, 0:width] + part[:, c : c + width]
        return carry

    lax.fori_loop(0, blocks // step, next_layers, 0)

    k = lax.broadcasted_iota(jnp.int32, (256, cols), 0)
    w = lax.broadcasted_iota(jnp.int32, (256, cols), 1)
    total = 0.0
    for d in range(4):
        sel = jnp.where(w == 2 * k - 3 + d, 1.0, 0.0).astype(BF16)
        lines = jnp.concatenate(
            [
                jnp.concatenate(
                    [acc[c, pl.ds(24 + 2 * d + ch, rows, stride=8), :] for c in range(2)], axis=1
                )
                for ch in range(2)
            ],
            axis=0,
        )
        total += mm(jnp.concatenate(split3(lines), axis=1), jnp.concatenate([sel] * 3, axis=0))
    for ch in range(2):
        part = total[ch * rows : (ch + 1) * rows]
        pred[ch] = part
        clean[ch] = (center[ch] - SIGMA_NOW * part) / SCALE_NOW


def run_network(noisy, top, bottom, side, flags, weights):
    _, rows, cols = noisy.shape
    blocks = rows // 2 + 2
    groups = -(-blocks // 4)
    used = ceil_to(cols // 2 + 2, 16)
    vmem = pl.BlockSpec(memory_space=pltpu.VMEM)
    shape = jax.ShapeDtypeStruct(noisy.shape, F32)
    return pl.pallas_call(
        network_kernel,
        out_shape=(shape, shape),
        in_specs=[pl.BlockSpec(memory_space=pltpu.SMEM)] + [vmem] * 7,
        out_specs=(vmem, vmem),
        scratch_shapes=[
            pltpu.VMEM((2, rows + 16, cols), F32),
            pltpu.VMEM((8, 8 * groups + 8, 256), F32),
            pltpu.VMEM((4 * groups + 1, used, 256), BF16),
            pltpu.VMEM((4 * groups + 1, used, 256), BF16),
            pltpu.VMEM((2, 16 * blocks + 16, 128), F32),
        ],
        cost_estimate=pl.CostEstimate(
            flops=20 * rows * cols * 64 * 64, bytes_accessed=24 * rows * cols, transcendentals=0
        ),
        name="network",
    )(flags, top, noisy, bottom, side, *weights)


def halo(noisy):
    gz = lax.axis_size("gz")
    _, rows, cols = noisy.shape
    left, right = noisy[:, :, :EDGE], noisy[:, :, cols - EDGE :]
    side = swap_cores(jnp.where(lax.axis_index("col") == 0, right, left))
    down = [(i, i + 1) for i in range(gz - 1)]
    lower = jnp.concatenate([noisy[:, rows - EDGE :], side[:, rows - EDGE :]], axis=2)
    upper = jnp.concatenate([noisy[:, :EDGE], side[:, :EDGE]], axis=2)
    top = lax.ppermute(lower, "gz", down)
    bottom = lax.ppermute(upper, "gz", [(b, a) for a, b in down])
    return top, bottom, side


def swap_cores(value):
    assert lax.axis_size("col") == 2
    return lax.ppermute(value, "col", [(0, 1), (1, 0)])


def edge_flags():
    row, col = lax.axis_index("gz"), lax.axis_index("col")
    last_row, last_col = lax.axis_size("gz") - 1, lax.axis_size("col") - 1
    return jnp.stack([row == 0, row == last_row, col == 0, col == last_col]).astype(jnp.int32)


def halves(matrix):
    high = matrix.astype(ml_dtypes.bfloat16)
    low = (matrix - high.astype(np.float64)).astype(ml_dtypes.bfloat16)
    return np.stack([high, low])


def fourier_parts(length, scale):
    index = np.arange(length)
    angle = 2.0 * np.pi * (np.outer(index, index) % length) / length
    return np.cos(angle) * scale, np.sin(angle) * scale


def turn_table(radix, inner):
    angle = 2.0 * np.pi * np.outer(np.arange(radix), np.arange(inner)) / (radix * inner)
    return np.stack([np.cos(angle), np.sin(angle)]).astype(np.float32)


def small_dft(values, sign):
    n = len(values)
    if n == 1:
        return values
    if n % 2 == 0:
        even = small_dft(values[0::2], sign)
        odd = small_dft(values[1::2], sign)
        low, high = [], []
        for q in range(n // 2):
            re, im = times_unit(odd[q], q, n, sign)
            low.append((even[q][0] + re, even[q][1] + im))
            high.append((even[q][0] - re, even[q][1] - im))
        return low + high
    if n == 3:
        (r0, i0), (r1, i1), (r2, i2) = values
        sr, si = r1 + r2, i1 + i2
        half = math.sqrt(3.0) / 2.0 * sign
        dr, di = half * (r1 - r2), half * (i1 - i2)
        tr, ti = r0 - 0.5 * sr, i0 - 0.5 * si
        return [(r0 + sr, i0 + si), (tr - di, ti + dr), (tr + di, ti - dr)]
    out = []
    for q in range(n):
        terms = [times_unit(v, a * q, n, sign) for a, v in enumerate(values)]
        out.append((sum(t[0] for t in terms), sum(t[1] for t in terms)))
    return out


def times_unit(value, power, n, sign):
    re, im = value
    power %= n
    if power == 0:
        return re, im
    if 4 * power == n:
        return (-im, re) if sign > 0 else (im, -re)
    if 2 * power == n:
        return -re, -im
    if 4 * power == 3 * n:
        return (im, -re) if sign > 0 else (-im, re)
    c = math.cos(2.0 * math.pi * power / n)
    s = sign * math.sin(2.0 * math.pi * power / n)
    return c * re - s * im, c * im + s * re


def turn(value, cos, sin, sign):
    re, im = value
    if sign > 0:
        return re * cos - im * sin, im * cos + re * sin
    return re * cos + im * sin, im * cos - re * sin


def beside(parts, axis):
    return jnp.concatenate([parts[0], parts[0], parts[1]], axis=axis)


def against(matrix, axis):
    return jnp.concatenate([matrix[0], matrix[1], matrix[0]], axis=axis)


def columns_forward_kernel(first, mine, other, maps, scales, matrix, table, out):
    radix, inner = table.shape[1:]
    coils = maps.shape[0]
    rows, cols = mine.shape[1:]
    groups = out.shape[0]
    per = inner // groups
    lead = first[0] != 0
    image = [
        jnp.concatenate(
            [jnp.where(lead, mine[p], other[p]), jnp.where(lead, other[p], mine[p])], axis=1
        )
        * scales[0:1, 0:1]
        for p in range(2)
    ]
    turned = []
    for coil in range(coils):
        maps_real, maps_imag = maps[coil, 0], maps[coil, 1]
        coil_image = (
            maps_real * image[0] - maps_imag * image[1],
            maps_real * image[1] + maps_imag * image[0],
        )
        parts = [
            tuple(v[:, a * inner : (a + 1) * inner] for v in coil_image) for a in range(radix)
        ]
        parts = small_dft(parts, -1)
        turned.append(
            [
                turn(part, table[0, q : q + 1, :], table[1, q : q + 1, :], -1) if q else part
                for q, part in enumerate(parts)
            ]
        )
    for q in range(radix):
        data = jnp.concatenate([jnp.concatenate(turned[c][q], axis=1) for c in range(coils)], axis=0)
        result = mm_nt(against(matrix, 1), beside(split2(data), 1))
        for p in range(2):
            for g in range(groups):
                start = p * inner + g * per
                for c in range(coils):
                    out[g, p, c, q] = result[start : start + per, c * rows : (c + 1) * rows]


def columns_forward(first, mine, other, maps, scales, groups, chunk, chunks):
    coils, _, rows, cols = maps.shape
    coils //= chunks
    inner = INNER
    radix = cols // inner
    c, s = fourier_parts(inner, 1.0 / math.sqrt(cols))
    matrix = halves(np.block([[c, s], [-s, c]]))
    table = turn_table(radix, inner)
    vmem = pl.BlockSpec(memory_space=pltpu.VMEM)
    per = inner // groups
    return pl.pallas_call(
        columns_forward_kernel,
        out_shape=jax.ShapeDtypeStruct((groups, 2, coils, radix, per, rows), F32),
        grid=(1,),
        in_specs=[
            pl.BlockSpec(memory_space=pltpu.SMEM),
            vmem,
            vmem,
            pl.BlockSpec((coils, 2, rows, cols), lambda i: (chunk, 0, 0, 0)),
            vmem,
            vmem,
            vmem,
        ],
        out_specs=pl.BlockSpec(
            (groups, 2, coils, radix, per, rows), lambda i: (0, 0, 0, 0, 0, 0)
        ),
        cost_estimate=pl.CostEstimate(
            flops=24 * coils * rows * cols * inner,
            bytes_accessed=16 * coils * rows * cols,
            transcendentals=0,
        ),
        name="columns_forward",
    )(first, mine, other, maps, scales, jnp.asarray(matrix), jnp.asarray(table))


def rows_kernel(data, kept, target, scales, forward, inverse, table, out, lines):
    radix = table.shape[1]
    count = data.shape[2]
    parts = small_dft([(data[a, 0], data[a, 1]) for a in range(radix)], -1)
    for q, part in enumerate(parts):
        if q:
            part = turn(part, table[0, q : q + 1, :], table[1, q : q + 1, :], -1)
        for p in range(2):
            lines[q * count : (q + 1) * count, p * LANES : (p + 1) * LANES] = part[p]
    spectrum = mm(beside(split2(lines[...]), 1), against(forward, 0))
    keep = kept[...].reshape(radix * count, LANES) * scales[2:3, :]
    unit = scales[1:2, :]
    residual = jnp.concatenate(
        [
            keep
            * (spectrum[:, p * LANES : (p + 1) * LANES] * unit - target[p].reshape(-1, LANES))
            for p in range(2)
        ],
        axis=1,
    )
    lines[...] = mm(beside(split2(residual), 1), against(inverse, 0))
    back = []
    for q in range(radix):
        part = tuple(
            lines[q * count : (q + 1) * count, p * LANES : (p + 1) * LANES] for p in range(2)
        )
        if q:
            part = turn(part, table[0, q : q + 1, :], table[1, q : q + 1, :], 1)
        back.append(part)
    for a, (re, im) in enumerate(small_dft(back, 1)):
        out[a, 0] = re
        out[a, 1] = im


def rows_both_ways(data, kept, target, scales, first_line):
    radix, _, count, _ = data.shape
    pencil = kept.shape[1]
    c, s = fourier_parts(LANES, 1.0 / math.sqrt(radix * LANES))
    forward = halves(np.block([[c, -s], [s, c]]))
    inverse = halves(np.block([[c, s], [-s, c]]))
    table = turn_table(radix, LANES)
    block = max(b for b in range(8, 56, 8) if pencil % b == 0)
    offset, repeat = first_line // block, pencil // block
    vmem = pl.BlockSpec(memory_space=pltpu.VMEM)
    spec = pl.BlockSpec((radix, 2, block, LANES), lambda i: (0, 0, i, 0))
    return pl.pallas_call(
        rows_kernel,
        out_shape=jax.ShapeDtypeStruct(data.shape, F32),
        grid=(count // block,),
        in_specs=[
            spec,
            pl.BlockSpec((radix, block, LANES), lambda i: (0, lax.rem(i + offset, repeat), 0)),
            pl.BlockSpec((2, radix, block, LANES), lambda i: (0, 0, i + offset, 0)),
            vmem,
            vmem,
            vmem,
            vmem,
        ],
        out_specs=spec,
        scratch_shapes=[pltpu.VMEM((radix * block, 2 * LANES), F32)],
        cost_estimate=pl.CostEstimate(
            flops=24 * radix * count * LANES * LANES,
            bytes_accessed=32 * radix * count * LANES,
            transcendentals=0,
        ),
        name="rows_both_ways",
    )(data, kept, target, scales, jnp.asarray(forward), jnp.asarray(inverse), jnp.asarray(table))


def columns_inverse_kernel(last, first, data, maps, scales, matrix, table, *refs):
    radix, inner = table.shape[1:]
    groups = data.shape[0]
    coils, _, rows, cols = maps.shape
    base, outs = (None, refs) if len(refs) == 1 else (refs[0], refs[1:])
    parts = []
    for q in range(radix):
        lines = jnp.concatenate(
            [
                jnp.transpose(
                    jnp.concatenate(
                        [data[g, p, c, q] for p in range(2) for g in range(groups)], axis=0
                    )
                )
                for c in range(coils)
            ],
            axis=0,
        )
        result = mm(beside(split2(lines), 1), against(matrix, 0))
        part = (result[:, :inner], result[:, inner:])
        if q:
            part = turn(part, table[0, q : q + 1, :], table[1, q : q + 1, :], 1)
        parts.append(part)
    sums = [[], []]
    for a, (re, im) in enumerate(small_dft(parts, 1)):
        where = slice(a * inner, (a + 1) * inner)
        total = [0.0, 0.0]
        for c in range(coils):
            maps_real, maps_imag = maps[c, 0, :, where], maps[c, 1, :, where]
            x, y = re[c * rows : (c + 1) * rows], im[c * rows : (c + 1) * rows]
            total[0] += maps_real * x + maps_imag * y
            total[1] += maps_real * y - maps_imag * x
        for p in range(2):
            part = total[p] * scales[3:4, 0:1]
            sums[p].append(part if base is None else base[p, :, where] + part)
    lead = first[0] != 0
    for p in range(2):
        line = jnp.concatenate(sums[p], axis=1)
        if last:
            own, away = line[:, : cols // 2], line[:, cols // 2 :]
            outs[0][p] = jnp.where(lead, own, away)
            outs[1][p] = jnp.where(lead, away, own)
        else:
            outs[0][p] = line


def columns_inverse(first, data, maps, scales, chunk, chunks, base):
    groups, _, coils, radix, per, rows = data.shape
    cols = maps.shape[3]
    inner = cols // radix
    c, s = fourier_parts(inner, 1.0 / math.sqrt(cols))
    matrix = halves(np.block([[c, s], [-s, c]]))
    table = turn_table(radix, inner)
    vmem = pl.BlockSpec(memory_space=pltpu.VMEM)
    last = chunk == chunks - 1
    if last:
        shape = [jax.ShapeDtypeStruct((2, rows, cols // 2), F32)] * 2
    else:
        shape = [jax.ShapeDtypeStruct((2, rows, cols), F32)]
    return pl.pallas_call(
        partial(columns_inverse_kernel, last),
        out_shape=shape,
        grid=(1,),
        in_specs=[
            pl.BlockSpec(memory_space=pltpu.SMEM),
            vmem,
            pl.BlockSpec((coils, 2, rows, cols), lambda i: (chunk, 0, 0, 0)),
            vmem,
            vmem,
            vmem,
        ]
        + [vmem] * len(base),
        out_specs=[vmem] * len(shape),
        cost_estimate=pl.CostEstimate(
            flops=24 * coils * rows * cols * inner,
            bytes_accessed=16 * coils * rows * cols,
            transcendentals=0,
        ),
        name="columns_inverse",
    )(first, data, maps, scales, jnp.asarray(matrix), jnp.asarray(table), *base)


def target_kernel(radix3, token, *refs):
    tiles = (len(refs) - 4) // 2
    measured, sampled = refs[:tiles], refs[tiles : 2 * tiles]
    target, kept, lines, order = refs[2 * tiles :]
    radix, pencil, _ = kept.shape
    count, height = lines.shape
    coils = count // pencil
    per = pencil // radix3

    @pl.when(pl.program_id(0) == 0)
    def _():
        source = lax.broadcasted_iota(jnp.int32, (height, LANES), 0)
        place = lax.broadcasted_iota(jnp.int32, (height, LANES), 1)
        for q in range(radix):
            order[:, q * LANES : (q + 1) * LANES] = jnp.where(
                source == radix * place + q, 1.0, 0.0
            ).astype(BF16)
        for t in range(tiles):
            for q in range(radix3):
                lines[q * per : (q + 1) * per, t * LANES : (t + 1) * LANES] = sampled[t][
                    pl.ds(q, per, stride=radix3), :
                ].astype(F32)
        picked = mm(lines[0:pencil, :].astype(BF16), order[...])
        for q in range(radix):
            kept[q] = picked[:, q * LANES : (q + 1) * LANES]

    for t in range(tiles):
        source = measured[t].reshape(count, LANES)
        for c in range(coils):
            for q in range(radix3):
                start = c * pencil + q * per
                lines[start : start + per, t * LANES : (t + 1) * LANES] = source[
                    pl.ds(q * coils + c, per, stride=radix3 * coils), :
                ]
    high, low = split2(lines[...])
    for q in range(0, radix, 2):
        width = min(2, radix - q) * LANES
        part = order[:, q * LANES : q * LANES + width]
        picked = mm(high, part) + mm(low, part)
        for k in range(0, width, LANES):
            target[0, q + k // LANES] = picked[:, k : k + LANES]


def prepare_target(token, measured, sampled, radix3):
    _, pencil, coils, height = measured.shape
    radix = height // LANES
    count = pencil * coils
    return pl.pallas_call(
        partial(target_kernel, radix3),
        out_shape=(
            jax.ShapeDtypeStruct((2, radix, count, LANES), F32),
            jax.ShapeDtypeStruct((radix, pencil, LANES), F32),
        ),
        grid=(2,),
        in_specs=[pl.BlockSpec(memory_space=pltpu.SMEM)]
        + [
            pl.BlockSpec((1, pencil, coils, LANES), lambda i, t=t: (i, 0, 0, t))
            for t in range(radix)
        ]
        + [pl.BlockSpec((pencil, LANES), lambda i, t=t: (0, t)) for t in range(radix)],
        out_specs=(
            pl.BlockSpec((1, radix, count, LANES), lambda i: (i, 0, 0, 0)),
            pl.BlockSpec((radix, pencil, LANES), lambda i: (0, 0, 0)),
        ),
        scratch_shapes=[pltpu.VMEM((count, height), F32), pltpu.VMEM((height, height), BF16)],
        cost_estimate=pl.CostEstimate(
            flops=8 * count * height * height, bytes_accessed=16 * count * height, transcendentals=0
        ),
        name="target",
    )(token, *[measured] * radix, *[sampled] * radix)


def exchange(value):
    return lax.all_to_all(value, "gz", split_axis=0, concat_axis=0, tiled=True)


def after(value, *earlier):
    return lax.optimization_barrier((value, *earlier))[0]


def local(
    noisy_image, fresh_noise, coil_maps, measured, sampled, first_kernel, inner_kernels, last_kernel
):
    groups = lax.axis_size("gz")
    coils, _, rows, cols = coil_maps.shape
    height = measured.shape[3]
    radix, inner = cols // INNER, INNER
    per = inner // groups
    row_radix = height // LANES
    chunks = 2
    pencil = radix * per
    count = coils * pencil // chunks
    lead = (lax.axis_index("col") == 0).astype(jnp.int32)[None]

    weights, scales = network_weights(
        first_kernel, inner_kernels[0], last_kernel, cols, height
    )
    top, bottom, side = halo(noisy_image)
    predicted, clean = run_network(noisy_image, top, bottom, side, edge_flags(), weights)
    other = swap_cores(clean)

    token = lead
    arrived = []
    for chunk in range(chunks):
        spectra = columns_forward(token, clean, other, coil_maps, scales, groups, chunk, chunks)
        spectra = spectra.reshape(groups, 2, count, rows).astype(jnp.float16)
        if chunk == 0:
            target, kept = prepare_target(after(lead, spectra), measured, sampled, radix)
            token = after(lead, kept)
        arrived.append(exchange(spectra))

    back = []
    for chunk in range(chunks):
        lines = after(arrived[chunk], *back).astype(F32)
        if rows != LANES:
            lines = jnp.transpose(lines, (1, 2, 0, 3)).reshape(2, -1, row_radix, LANES)
            lines = jnp.transpose(lines, (2, 0, 1, 3))
        lines = rows_both_ways(lines, kept, target, scales, chunk * (coils // chunks) * pencil)
        if rows != LANES:
            lines = jnp.transpose(lines, (1, 2, 0, 3)).reshape(2, -1, groups, rows)
            lines = jnp.transpose(lines, (2, 0, 1, 3))
        back.append(lines.astype(jnp.float16))

    gradient = []
    for chunk in range(chunks):
        lines = after(exchange(back[chunk]), *gradient).astype(F32)
        lines = lines.reshape(groups, 2, coils // chunks, radix, per, rows)
        gradient = columns_inverse(lead, lines, coil_maps, scales, chunk, chunks, gradient)

    own, away = gradient
    own = own + swap_cores(away)
    update = clean - STEP_GAIN * own
    return SCALE_NEXT * update + DIRECT_GAIN * predicted + NOISE_GAIN * fresh_noise


def solution(mesh):
    in_specs = (
        P("grp", "gz", "col"),
        P("grp", "gz", "col"),
        P("col", "grp", "gz", None),
        P("grp", "gz", "col", None),
        P("gz", "grp"),
        P(),
        P(),
        P(),
    )
    out_specs = P("grp", "gz", "col")
    return jax.shard_map(local, mesh=mesh, in_specs=in_specs, out_specs=out_specs, check_vma=False)
```

time: 194 us -> 160 us (0.82)
  waiting for transfers between devices: 61.7 us -> 46 us
  local copies, waits for them, and re-layouts: 12.9 us -> 2.13 us
  Pallas kernels: 77.7 us -> 68.7 us
  other arithmetic: 14.6 us -> 18.8 us
  between operations: 2.64 us -> 0.08 us
    all_to_all x2 -> x4, waiting for transfers between devices: 60 us -> 40.3 us  [exchange(): return lax.all_to_all(value, 'gz', split_axis=0, concat_axis=0, tiled=True)]
    pallas_call x1, Pallas kernels: 39.3 us -> 26.6 us  [run_network(): pl.pallas_call(network_kernel, out_shape=(shape, shape), in_specs=[pl.Blo...]
    reshape x3 -> x0, local copies, waits for them, and re-layouts: 7.51 us -> none  [the longest x1 4.92 us: prepare_target(): measured = measured.reshape(2, count, height)]
    all_to_all x2 -> x4, starting transfers between devices: 9.99 us -> 16.5 us  [exchange(): return lax.all_to_all(value, 'gz', split_axis=0, concat_axis=0, tiled=True)]
    ppermute x7 -> x5, starting transfers between devices: 12.9 us -> 6.63 us  [the longest x1 4.77 us: halo(): top = lax.ppermute(lower, 'gz', down)]
    convert_element_type x2 -> x6, other arithmetic: 6.9 us -> 12.5 us  [the longest x2 4.97 us: local(): spectra = spectra.reshape(groups, 2, count, rows).astype(jnp.float16)]
    ppermute x7 -> x5, waiting for transfers between devices: 1.73 us -> 5.64 us  [the longest x3 4.09 us: swap_cores(): return lax.ppermute(value, 'col', [(0, 1), (1, 0)])]
    mul x2 -> x0, other arithmetic: 3.85 us -> none  [exchange(): return half.astype(F32) * (bound / 60000.0)]
  transfers between devices with their start and end apart: 9 -> 9, of which waited for: 3 -> 8; matrix products, arithmetic and copies ran while one was open for 6% -> 8% of each run, Pallas kernels for 5% -> 20%
where the time goes in v3:
time: 160 us; the launch traced here: 159 us
  Pallas kernels  68.7 us (43%)
  waiting for transfers between devices  46 us (29%)
  starting transfers between devices  23.2 us (14%)
  other arithmetic  18.8 us (12%)
  local copies, waits for them, and re-layouts  2.13 us (1%)
    all_to_all x4, waiting for transfers between devices, exchange(): return lax.all_to_all(value, 'gz', split_axis=0, concat_axis=0, tiled=True)  40.3 us
    pallas_call x1, Pallas kernels, run_network(): pl.pallas_call(network_kernel, out_shape=(shape, shape), in_specs=[pl.Blo...  26.6 us
    all_to_all x4, starting transfers between devices, exchange(): return lax.all_to_all(value, 'gz', split_axis=0, concat_axis=0, tiled=True)  16.5 us
    pallas_call x2, Pallas kernels, rows_both_ways(): pl.pallas_call(rows_kernel, out_shape=jax.ShapeDtypeStruct(data.shape, F3...  12.3 us
    pallas_call x2, Pallas kernels, columns_inverse(): pl.pallas_call(partial(columns_inverse_kernel, last), out_shape=shape, gr...  10.1 us
    pallas_call x2, Pallas kernels, columns_forward(): pl.pallas_call(columns_forward_kernel, out_shape=jax.ShapeDtypeStruct((gr...  9.7 us
    pallas_call x1, Pallas kernels, prepare_target(): pl.pallas_call(partial(target_kernel, radix3), out_shape=(jax.ShapeDtypeS...  7.61 us
    convert_element_type x2, other arithmetic, local(): spectra = spectra.reshape(groups, 2, count, rows).astype(jnp.float16)  4.97 us
  transfers between devices with their start and end apart: 9, of which 8 were waited for; matrix products, arithmetic and copies ran while one was open for 8% of the time, Pallas kernels for 20%

profile of v3, /device:TPU:0, one launch (start us, length us, event | category | flops | bytes accessed | tf_op | source)
XLA Modules:
  0.0 158.8 jit_solution(9861164194061835554)
XLA Ops:
  0.0 1.1 slice_select_fusion
  1.1 0.6 collective-permute-start
  1.6 0.8 fusion
  2.4 0.2 collective-permute-done.side
  2.6 0.0 copy-start.4
  2.6 4.8 %collective-permute-start.1 = (f32[2,8,392]{2,1,0:T(8,128)S(1)}, f32[2,8,392]{2,1,0:T(8,128)S(1)}, u32[]{:S(2)}, u32[]{:S(2)}) collective-permute-start(f32[2,8,392]{2,1,0:T(8,128)S(1)} %pad_maximum_fusion), channel_id=1, source_target_pairs={{0,2},{2,4},{4,6},{6,8},{8,10},{10,12},{12,14},{1,3},{3,5},{5,7},{... | collective-permute-start | bytes 75272 | tf_op jit(solution)/shard_map/ppermute | solution.py:308
  7.4 1.3 collective-permute-start.2
  8.7 0.6 add_convert_fusion.flags
  9.3 2.4 %weights.1 = (bf16[4,128,256]{2,1,0:T(8,128)(2,1)}, bf16[1024,256]{1,0:T(8,128)(2,1)}, bf16[32,256]{1,0:T(8,128)(2,1)}, f32[8,128]{1,0:T(8,128)}) custom-call(bf16[9,2,64]{2,1,0:T(2,128)(2,1)} %bitcast.15, bf16[9,64,64]{2,1,0:T(8,128)(2,1)} %bitcast.14, bf16[9,2,64]{2,1,0:T(2,128)(2,1)} %last_taps.1, bf16[4,512,18]{2,1,0:T(8,128)(2,1)} %constant.34.clone.choice1, ...), custom_call_target="tpu_custom_call" | custom-call | flops 10000000 | bytes 1000000 | tf_op jit(solution)/shard_map/weights/pallas_call | solution.py:109
  11.7 0.0 collective-permute-done.1.top
  11.7 0.0 copy-start.5
  11.7 1.5 collective-permute-done.2.bottom
  13.2 0.0 copy-start.6
  13.2 0.0 copy-done.4
  13.2 0.0 copy-done.5
  13.2 0.6 copy-done.6
  13.8 26.6 %network.1 = (f32[2,128,384]{2,1,0:T(8,128)}, f32[2,128,384]{2,1,0:T(8,128)}) custom-call(s32[4]{0:T(128)} %add_convert_fusion.flags, f32[2,8,392]{2,1,0:T(8,128)} %copy-done.5, f32[2,128,384]{2,1,0:T(8,128)} %center.1, f32[2,8,392]{2,1,0:T(8,128)} %copy-done.6, f32[2,128,8]{2,1,0:T(8,128)} %copy-done.4, bf16[4,128,256]{2,1,0:T(8,128)(2,1)} %get-tuple-element.19.first, ...), custom_call_target="tpu_custom_call" | custom-call | flops 4026531840 | bytes 1179648 | tf_op jit(solution)/shard_map/network/pallas_call | solution.py:281
  40.5 0.0 collective-permute-start.3
  40.5 1.9 %collective-permute-done.3.other = f32[2,128,384]{2,1,0:T(8,128)S(1)} collective-permute-done((f32[2,128,384]{2,1,0:T(8,128)}, f32[2,128,384]{2,1,0:T(8,128)S(1)}, u32[]{:S(2)}, u32[]{:S(2)}) %collective-permute-start.3) | collective-permute-done | bytes 393248 | tf_op jit(solution)/shard_map/ppermute | solution.py:315
  42.4 0.0 copy-start.1
  42.4 0.8 copy-done.1
  43.2 4.9 %columns_forward.2 = f32[8,2,2,3,32,128]{5,4,3,2,1,0:T(8,128)} custom-call(s32[1]{0:T(128)S(6)} %broadcast_in_dim.3.first.token, f32[2,128,384]{2,1,0:T(8,128)} %get-tuple-element.22.mine, f32[2,128,384]{2,1,0:T(8,128)} %copy-done.1, f32[4,2,128,768]{3,2,1,0:T(8,128)} %maps.7, f32[8,128]{1,0:T(8,128)} %get-tuple-element.23.scales, ...), custom_call_target="tpu_custom_call" | custom-call | flops 1207959552 | bytes 3145728 | tf_op jit(solution)/shard_map/columns_forward/pallas_call | solution.py:450
  48.0 2.5 %convert_element_type.31 = f16[8,2,2,3,32,128]{5,4,3,2,1,0:T(8,128)(2,1)} convert(f32[8,2,2,3,32,128]{5,4,3,2,1,0:T(8,128)} %columns_forward.2) | non-fusion elementwise | flops 393216 | bytes 2359296 | tf_op jit(solution)/shard_map/convert_element_type | solution.py:731
  50.5 5.7 %all-to-all-start.1 = ((f16[8,2,192,128]{3,2,1,0:T(8,128)(2,1)}), f16[8,2,192,128]{3,2,1,0:T(8,128)(2,1)S(1)}, u32[]{:S(2)}, u32[]{:S(2)}) async-start(f16[8,2,192,128]{3,2,1,0:T(8,128)(2,1)} %bitcast.6), calls=%async_computation.1 | async-start | bytes 1572864 | tf_op jit(solution)/shard_map/all_to_all | solution.py:699
  56.2 7.6 %target.1 = (f32[2,8,384,128]{3,2,1,0:T(8,128)}, f32[8,96,128]{2,1,0:T(8,128)}) custom-call(s32[1]{0:T(128)S(6)} %broadcast_in_dim.3.first.token, f32[2,96,4,1024]{3,2,1,0:T(4,128)} %refs_7_.1, f32[2,96,4,1024]{3,2,1,0:T(4,128)} %refs_7_.1, f32[2,96,4,1024]{3,2,1,0:T(4,128)} %refs_7_.1, f32[2,96,4,1024]{3,2,1,0:T(4,128)} %refs_7_.1, ...), custom_call_target="tpu_custom_call" | custom-call | flops 3221225472 | bytes 6291456 | tf_op jit(solution)/shard_map/target/pallas_call | solution.py:673
  63.8 4.9 %columns_forward.3 = f32[8,2,2,3,32,128]{5,4,3,2,1,0:T(8,128)} custom-call(s32[1]{0:T(128)S(6)} %broadcast_in_dim.3.first.token, f32[2,128,384]{2,1,0:T(8,128)} %get-tuple-element.22.mine, f32[2,128,384]{2,1,0:T(8,128)} %copy-done.1, f32[4,2,128,768]{3,2,1,0:T(8,128)} %maps.7, f32[8,128]{1,0:T(8,128)} %get-tuple-element.23.scales, ...), custom_call_target="tpu_custom_call" | custom-call | flops 1207959552 | bytes 3145728 | tf_op jit(solution)/shard_map/columns_forward/pallas_call | solution.py:450
  68.7 2.5 %convert_element_type.33 = f16[8,2,2,3,32,128]{5,4,3,2,1,0:T(8,128)(2,1)} convert(f32[8,2,2,3,32,128]{5,4,3,2,1,0:T(8,128)} %columns_forward.3) | non-fusion elementwise | flops 393216 | bytes 2359296 | tf_op jit(solution)/shard_map/convert_element_type | solution.py:731
  71.1 5.5 %all-to-all-done.1 = f16[8,2,192,128]{3,2,1,0:T(8,128)(2,1)S(1)} async-done(((f16[8,2,192,128]{3,2,1,0:T(8,128)(2,1)}), f16[8,2,192,128]{3,2,1,0:T(8,128)(2,1)S(1)}, u32[]{:S(2)}, u32[]{:S(2)}) %all-to-all-start.1) | async-done | bytes 786464 | tf_op jit(solution)/shard_map/all_to_all | solution.py:699
  76.6 3.6 %all-to-all-start = ((f16[8,2,192,128]{3,2,1,0:T(8,128)(2,1)}), f16[8,2,192,128]{3,2,1,0:T(8,128)(2,1)S(1)}, u32[]{:S(2)}, u32[]{:S(2)}) async-start(f16[8,2,192,128]{3,2,1,0:T(8,128)(2,1)} %bitcast.7), calls=%async_computation | async-start | bytes 1572864 | tf_op jit(solution)/shard_map/all_to_all | solution.py:699
  80.2 1.3 convert_element_type.35.data
  81.6 6.1 %rows_both_ways.2 = f32[8,2,192,128]{3,2,1,0:T(8,128)} custom-call(f32[8,2,192,128]{3,2,1,0:T(8,128)} %convert_element_type.35.data, f32[8,96,128]{2,1,0:T(8,128)} %get-tuple-element.25.kept, f32[2,8,384,128]{3,2,1,0:T(8,128)} %get-tuple-element.27.target, f32[8,128]{1,0:T(8,128)} %get-tuple-element.23.scales, bf16[2,256,256]{2,1,0:T(8,128)(2,1)} %constant.38.clone.forward, ...), custom_call_target="tpu_custom_call" | custom-call | flops 603979776 | bytes 6291456 | tf_op jit(solution)/shard_map/rows_both_ways/pallas_call | solution.py:520
  87.7 2.5 %convert_element_type.36 = f16[8,2,192,128]{3,2,1,0:T(8,128)(2,1)} convert(f32[8,2,192,128]{3,2,1,0:T(8,128)} %rows_both_ways.2) | non-fusion elementwise | flops 393216 | bytes 2359296 | tf_op jit(solution)/shard_map/convert_element_type | solution.py:747
  90.1 10.5 %all-to-all-done = f16[8,2,192,128]{3,2,1,0:T(8,128)(2,1)S(1)} async-done(((f16[8,2,192,128]{3,2,1,0:T(8,128)(2,1)}), f16[8,2,192,128]{3,2,1,0:T(8,128)(2,1)S(1)}, u32[]{:S(2)}, u32[]{:S(2)}) %all-to-all-start) | async-done | bytes 786464 | tf_op jit(solution)/shard_map/all_to_all | solution.py:699
  100.6 3.5 %all-to-all-start.3 = ((f16[8,2,192,128]{3,2,1,0:T(8,128)(2,1)}), f16[8,2,192,128]{3,2,1,0:T(8,128)(2,1)S(1)}, u32[]{:S(2)}, u32[]{:S(2)}) async-start(f16[8,2,192,128]{3,2,1,0:T(8,128)(2,1)} %convert_element_type.36), calls=%async_computation.3 | async-start | bytes 1572864 | tf_op jit(solution)/shard_map/all_to_all | solution.py:699
  104.2 1.3 convert_element_type.37.data
  105.5 6.1 %rows_both_ways.3 = f32[8,2,192,128]{3,2,1,0:T(8,128)} custom-call(f32[8,2,192,128]{3,2,1,0:T(8,128)} %convert_element_type.37.data, f32[8,96,128]{2,1,0:T(8,128)} %get-tuple-element.25.kept, f32[2,8,384,128]{3,2,1,0:T(8,128)} %get-tuple-element.27.target, f32[8,128]{1,0:T(8,128)} %get-tuple-element.23.scales, bf16[2,256,256]{2,1,0:T(8,128)(2,1)} %constant.38.clone.forward, ...), custom_call_target="tpu_custom_call" | custom-call | flops 603979776 | bytes 6291456 | tf_op jit(solution)/shard_map/rows_both_ways/pallas_call | solution.py:520
  111.6 2.5 %convert_element_type.38 = f16[8,2,192,128]{3,2,1,0:T(8,128)(2,1)} convert(f32[8,2,192,128]{3,2,1,0:T(8,128)} %rows_both_ways.3) | non-fusion elementwise | flops 393216 | bytes 2359296 | tf_op jit(solution)/shard_map/convert_element_type | solution.py:747
  114.1 10.5 %all-to-all-done.3 = f16[8,2,192,128]{3,2,1,0:T(8,128)(2,1)S(1)} async-done(((f16[8,2,192,128]{3,2,1,0:T(8,128)(2,1)}), f16[8,2,192,128]{3,2,1,0:T(8,128)(2,1)S(1)}, u32[]{:S(2)}, u32[]{:S(2)}) %all-to-all-start.3) | async-done | bytes 786464 | tf_op jit(solution)/shard_map/all_to_all | solution.py:699
  124.5 3.7 %all-to-all-start.2 = ((f16[8,2,192,128]{3,2,1,0:T(8,128)(2,1)}), f16[8,2,192,128]{3,2,1,0:T(8,128)(2,1)S(1)}, u32[]{:S(2)}, u32[]{:S(2)}) async-start(f16[8,2,192,128]{3,2,1,0:T(8,128)(2,1)} %convert_element_type.38), calls=%async_computation.2 | async-start | bytes 1572864 | tf_op jit(solution)/shard_map/all_to_all | solution.py:699
  128.3 1.4 convert.3.data
  129.7 4.9 %columns_inverse.2.refs_0_ = f32[2,128,768]{2,1,0:T(8,128)} custom-call(s32[1]{0:T(128)S(6)} %broadcast_in_dim.3.first.token, f32[8,2,2,3,32,128]{5,4,3,2,1,0:T(8,128)} %convert.3.data, f32[4,2,128,768]{3,2,1,0:T(8,128)} %maps.7, f32[8,128]{1,0:T(8,128)} %get-tuple-element.23.scales, bf16[2,512,512]{2,1,0:T(8,128)(2,1)} %constant.36.clone.matrix, ...), custom_call_target="tpu_custom_call" | custom-call | flops 1207959552 | bytes 3145728 | tf_op jit(solution)/shard_map/columns_inverse/pallas_call | solution.py:603
  134.5 13.9 %all-to-all-done.2 = f16[8,2,192,128]{3,2,1,0:T(8,128)(2,1)S(1)} async-done(((f16[8,2,192,128]{3,2,1,0:T(8,128)(2,1)}), f16[8,2,192,128]{3,2,1,0:T(8,128)(2,1)S(1)}, u32[]{:S(2)}, u32[]{:S(2)}) %all-to-all-start.2) | async-done | bytes 786464 | tf_op jit(solution)/shard_map/all_to_all | solution.py:699
  148.4 1.4 convert.4.data
  149.8 0.0 copy-start
  149.8 0.0 copy-start.2
  149.8 0.0 copy-start.3
  149.8 5.2 %columns_inverse.3 = (f32[2,128,384]{2,1,0:T(8,128)}, f32[2,128,384]{2,1,0:T(8,128)}) custom-call(s32[1]{0:T(128)S(6)} %broadcast_in_dim.3.first.token, f32[8,2,2,3,32,128]{5,4,3,2,1,0:T(8,128)} %convert.4.data, f32[4,2,128,768]{3,2,1,0:T(8,128)} %maps.7, f32[8,128]{1,0:T(8,128)} %get-tuple-element.23.scales, bf16[2,512,512]{2,1,0:T(8,128)(2,1)} %constant.36.clone.matrix, ...), custom_call_target="tpu_custom_call" | custom-call | flops 1207959552 | bytes 3145728 | tf_op jit(solution)/shard_map/columns_inverse/pallas_call | solution.py:603
  155.1 0.0 collective-permute-start.4
  155.1 1.9 %collective-permute-done.4 = f32[2,128,384]{2,1,0:T(8,128)S(1)} collective-permute-done((f32[2,128,384]{2,1,0:T(8,128)}, f32[2,128,384]{2,1,0:T(8,128)S(1)}, u32[]{:S(2)}, u32[]{:S(2)}) %collective-permute-start.4) | collective-permute-done | bytes 393248 | tf_op jit(solution)/shard_map/ppermute | solution.py:315
  157.0 0.0 copy-done
  157.0 0.0 copy-done.2
  157.0 0.0 copy-done.3
  157.0 1.9 %multiply_add_fusion = f32[2,128,384]{2,1,0:T(8,128)} fusion(f32[2,128,384]{2,1,0:T(8,128)S(1)} %copy-done.2, f32[2,128,384]{2,1,0:T(8,128)S(1)} %copy-done.3, f32[2,128,384]{2,1,0:T(8,128)S(1)} %copy-done, f32[2,128,384]{2,1,0:T(8,128)} %get-tuple-element.30, f32[2,128,384]{2,1,0:T(8,128)S(1)} %collective-permute-done.4), kind=kLoop, calls=%fused_computation | loop fusion | flops 688128 | bytes 2359296 | tf_op jit(solution)/shard_map/add | solution.py:758
  (3 shorter events, 0.0 us)
Async XLA Ops:
  1.1 1.5 collective-permute-start
  2.6 10.6 %copy-start.4 = (f32[2,128,8]{2,1,0:T(8,128)}, f32[2,128,8]{2,1,0:T(8,128)S(1)}, u32[]{:S(2)}) copy-start(f32[2,128,8]{2,1,0:T(8,128)S(1)} %collective-permute-done.side) | copy-start | bytes 24580
  2.6 9.0 %collective-permute-start.1 = (f32[2,8,392]{2,1,0:T(8,128)S(1)}, f32[2,8,392]{2,1,0:T(8,128)S(1)}, u32[]{:S(2)}, u32[]{:S(2)}) collective-permute-start(f32[2,8,392]{2,1,0:T(8,128)S(1)} %pad_maximum_fusion), channel_id=1, source_target_pairs={{0,2},{2,4},{4,6},{6,8},{8,10},{10,12},{12,14},{1,3},{3,5},{5,7},{... | collective-permute-start | bytes 75272 | tf_op jit(solution)/shard_map/ppermute | solution.py:308
  7.4 5.8 %collective-permute-start.2 = (f32[2,8,392]{2,1,0:T(8,128)S(1)}, f32[2,8,392]{2,1,0:T(8,128)S(1)}, u32[]{:S(2)}, u32[]{:S(2)}) collective-permute-start(f32[2,8,392]{2,1,0:T(8,128)S(1)} %pad_maximum_fusion.1), channel_id=1, source_target_pairs={{2,0},{4,2},{6,4},{8,6},{10,8},{12,10},{14,12},{3,1},{5,3},{7,5},{... | collective-permute-start | bytes 75272 | tf_op jit(solution)/shard_map/ppermute | solution.py:309
  11.7 1.6 copy-start.5
  13.2 0.6 copy-start.6
  40.5 1.9 %collective-permute-start.3 = (f32[2,128,384]{2,1,0:T(8,128)}, f32[2,128,384]{2,1,0:T(8,128)S(1)}, u32[]{:S(2)}, u32[]{:S(2)}) collective-permute-start(f32[2,128,384]{2,1,0:T(8,128)} %get-tuple-element.22.mine), channel_id=1, source_target_pairs={{0,1},{1,0},{2,3},{3,2},{4,5},{5,4},{6,7},{7,6},{8,9},{9,8},{10,11... | collective-permute-start | bytes 1179656 | tf_op jit(solution)/shard_map/ppermute | solution.py:315
  42.4 0.8 copy-start.1
  50.5 26.1 %all-to-all-start.1 = ((f16[8,2,192,128]{3,2,1,0:T(8,128)(2,1)}), f16[8,2,192,128]{3,2,1,0:T(8,128)(2,1)S(1)}, u32[]{:S(2)}, u32[]{:S(2)}) async-start(f16[8,2,192,128]{3,2,1,0:T(8,128)(2,1)} %bitcast.6), calls=%async_computation.1 | async-start | bytes 1572864 | tf_op jit(solution)/shard_map/all_to_all | solution.py:699
  76.6 24.0 %all-to-all-start = ((f16[8,2,192,128]{3,2,1,0:T(8,128)(2,1)}), f16[8,2,192,128]{3,2,1,0:T(8,128)(2,1)S(1)}, u32[]{:S(2)}, u32[]{:S(2)}) async-start(f16[8,2,192,128]{3,2,1,0:T(8,128)(2,1)} %bitcast.7), calls=%async_computation | async-start | bytes 1572864 | tf_op jit(solution)/shard_map/all_to_all | solution.py:699
  100.6 23.9 %all-to-all-start.3 = ((f16[8,2,192,128]{3,2,1,0:T(8,128)(2,1)}), f16[8,2,192,128]{3,2,1,0:T(8,128)(2,1)S(1)}, u32[]{:S(2)}, u32[]{:S(2)}) async-start(f16[8,2,192,128]{3,2,1,0:T(8,128)(2,1)} %convert_element_type.36), calls=%async_computation.3 | async-start | bytes 1572864 | tf_op jit(solution)/shard_map/all_to_all | solution.py:699
  124.5 23.9 %all-to-all-start.2 = ((f16[8,2,192,128]{3,2,1,0:T(8,128)(2,1)}), f16[8,2,192,128]{3,2,1,0:T(8,128)(2,1)S(1)}, u32[]{:S(2)}, u32[]{:S(2)}) async-start(f16[8,2,192,128]{3,2,1,0:T(8,128)(2,1)} %convert_element_type.38), calls=%async_computation.2 | async-start | bytes 1572864 | tf_op jit(solution)/shard_map/all_to_all | solution.py:699
  149.8 7.2 %copy-start = (f32[2,128,384]{2,1,0:T(8,128)S(1)}, f32[2,128,384]{2,1,0:T(8,128)}, u32[]{:S(2)}) copy-start(f32[2,128,384]{2,1,0:T(8,128)} %get-tuple-element.22.mine) | copy-start | bytes 1179652
  149.8 7.2 %copy-start.2 = (f32[2,128,384]{2,1,0:T(8,128)S(1)}, f32[2,128,384]{2,1,0:T(8,128)}, u32[]{:S(2)}) copy-start(f32[2,128,384]{2,1,0:T(8,128)} %param.25) | copy-start | bytes 1179652
  149.8 7.2 %copy-start.3 = (f32[2,128,384]{2,1,0:T(8,128)S(1)}, f32[2,128,384]{2,1,0:T(8,128)}, u32[]{:S(2)}) copy-start(f32[2,128,384]{2,1,0:T(8,128)} %get-tuple-element.32) | copy-start | bytes 1179652
  155.1 1.9 %collective-permute-start.4 = (f32[2,128,384]{2,1,0:T(8,128)}, f32[2,128,384]{2,1,0:T(8,128)S(1)}, u32[]{:S(2)}, u32[]{:S(2)}) collective-permute-start(f32[2,128,384]{2,1,0:T(8,128)} %get-tuple-element.31), channel_id=1, source_target_pairs={{0,1},{1,0},{2,3},{3,2},{4,5},{5,4},{6,7},{7,6},{8,9},{9,8},{10,11... | collective-permute-start | bytes 1179656 | tf_op jit(solution)/shard_map/ppermute | solution.py:315
